TPU v7x, 512 devices: a whole 4x8x8 slice. The times are simulated.
512 devices in a mesh: leaf: 8 (over z), row: 4 (over x), col: 16 (over y, core).
Axes of the slice: x: 4, y: 8, z: 8, core: 2. Of those that a mesh axis runs over, the one named last changes fastest.
Arguments:
- leaf_rhs: float32 [16, 16, 4096], P('leaf', None, 'col'), may hold values from -6 to 6
- leaf_inverse: float32 [16, 4096, 4096], P('leaf', 'row', 'col'), as said below
- update_rows: float32 [16, 2048, 4096], P('leaf', 'col', 'row'), may hold values from -0.09375 to 0.09375
- update_map: int32 [16, 16], P('leaf'), may hold values from 0 to 31, as said below
- sep_rhs: float32 [16, 4096], replicated, may hold values from -6 to 6
- sep_inverse: float32 [4096, 4096], P(('leaf', 'row', 'col')), as said below
Outputs:
- leaf_solution: float32 [16, 16, 4096], P('leaf', None, ('col', 'row'))
- sep_solution: float32 [16, 4096], P(None, ('leaf', 'row', 'col'))
Inputs may be any that keep to these rules, and one draw needn't show every extreme that they name: `update_map`: each row names 16 different separator blocks. `leaf_inverse`: entries off the diagonal are independent and of order 1 / sqrt(4096); each diagonal entry is one plus such a term. `sep_inverse`: entries off the diagonal are independent and of order 1 / sqrt(4096); each diagonal entry is one plus such a term.
All inputs are finite; a program needn't handle non-finite values.
Results may differ from a plain program's by a relative error of at most 0.000068.
Values sent between devices are 32-bit elements; how exact they have to be, the bound alone decides.
A program may use at most 64 MiB of HBM per device.

v0:
```python
import jax
import jax.numpy as jnp
from jax import lax
from jax.sharding import PartitionSpec as P

BLOCK = 128


HIGH = lax.Precision.HIGHEST


def body(leaf_rhs, leaf_inverse, update_rows, update_map, sep_rhs, sep_inverse):
    subs = leaf_rhs.shape[0]
    nrhs = leaf_rhs.shape[1]
    width = sep_rhs.shape[1]
    blocks_total = width // BLOCK
    blocks_here = update_rows.shape[1] // BLOCK
    first_block = lax.axis_index("col") * blocks_here
    local_map = lax.dynamic_slice_in_dim(update_map, first_block, blocks_here, 1)
    onehot = (
        local_map[:, :, None] == jnp.arange(blocks_total, dtype=jnp.int32)[None, None, :]
    ).astype(jnp.float32)
    partial_fwd = jnp.einsum("sij,srj->sri", leaf_inverse, leaf_rhs, precision=HIGH)
    forward = lax.psum(partial_fwd, "col")
    coupled = jnp.einsum("sun,srn->sru", update_rows, forward, precision=HIGH)
    coupled = coupled.reshape(subs, nrhs, blocks_here, BLOCK)
    contrib = jnp.einsum("srkc,skb->rbc", coupled, onehot, precision=HIGH).reshape(nrhs, width)
    sep_rows = sep_inverse.shape[0]
    row_start = lax.axis_index(("leaf", "row", "col")) * sep_rows
    total = lax.psum(contrib, ("leaf", "row", "col"))
    updated = sep_rhs - total
    sep_forward = jnp.einsum("ij,rj->ri", sep_inverse, updated, precision=HIGH)
    back_terms = jnp.einsum("ij,ri->rj", sep_inverse, sep_forward, precision=HIGH)
    sep_whole = lax.psum(back_terms, ("leaf", "row", "col"))
    sep_solution = lax.dynamic_slice_in_dim(sep_whole, row_start, sep_rows, 1)
    pulled = jnp.einsum(
        "rbc,skb->srkc", sep_whole.reshape(nrhs, blocks_total, BLOCK), onehot, precision=HIGH
    )
    pulled = pulled.reshape(subs, nrhs, blocks_here * BLOCK)
    pull_terms = jnp.einsum("sun,sru->srn", update_rows, pulled, precision=HIGH)
    pull_total = lax.psum(pull_terms, "col")
    reduced = forward - pull_total
    column_terms = jnp.einsum("sij,sri->srj", leaf_inverse, reduced, precision=HIGH)
    leaf_solution = lax.psum_scatter(column_terms, "row", scatter_dimension=2, tiled=True)
    return (leaf_solution, sep_solution)


def solution(mesh):
    in_specs = (
        P("leaf", None, "col"),
        P("leaf", "row", "col"),
        P("leaf", "col", "row"),
        P("leaf", None),
        P(),
        P(("leaf", "row", "col"), None),
    )
    out_specs = (P("leaf", None, ("col", "row")), P(None, ("leaf", "row", "col")))
    return jax.shard_map(body, mesh=mesh, in_specs=in_specs, out_specs=out_specs, check_vma=False)
```

profile of v0, /device:TPU:1, one launch (start us, length us, event | category | flops | bytes accessed | tf_op | source)
XLA Modules:
  0.0 832.1 jit_solution(7228872072157452738)
XLA Ops:
  7.2 0.0 copy-start
  7.2 0.0 copy-start.4
  7.2 0.0 copy-start.1
  7.2 0.0 copy-start.3
  7.2 0.0 all-reduce.5.cloned.1.call-start
  7.3 1.5 copy-done
  8.8 3.2 fusion.17
  12.0 0.0 all-reduce.5.cloned.1.call-update
  12.0 0.0 all-reduce.7.cloned.1.call-start
  12.1 0.0 copy-done.4
  12.1 0.2 dynamic-slice_reduce_fusion
  12.3 120.1 %all-reduce.5.cloned.1.call-done = f32[2,16,1024]{2,1,0:T(8,128)} async-done(((f32[2,16,1024]{2,1,0:T(8,128)}), f32[2,16,1024]{2,1,0:T(8,128)}) %all-reduce.5.cloned.1.call-update) | async-done | bytes 131088 | tf_op jit(solution)/shard_map/psum | solution.py:24
  132.4 0.0 copy-done.1
  132.4 1.9 fusion.18
  134.3 0.4 fusion.6
  134.7 0.0 copy-start.2
  134.7 0.9 copy.21
  135.6 0.0 all-reduce.7.cloned.1.call-update
  135.6 0.0 all-reduce.9.cloned.1.call-start
  135.7 274.1 %all-reduce.7.cloned.1.call-done = f32[16,4096]{1,0:T(8,128)} async-done(((f32[16,4096]{1,0:T(8,128)}), f32[16,4096]{1,0:T(8,128)}) %all-reduce.7.cloned.1.call-update) | async-done | bytes 262160 | tf_op jit(solution)/shard_map/psum | solution.py:30
  409.8 0.0 copy-done.3
  409.8 1.5 fusion
  411.3 1.1 fusion.19
  412.3 0.0 all-reduce.9.cloned.1.call-update
  412.4 0.0 all-reduce.11.cloned.1.call-start
  412.4 270.0 %all-reduce.9.cloned.1.call-done = f32[16,4096]{1,0:T(8,128)} async-done(((f32[16,4096]{1,0:T(8,128)}), f32[16,4096]{1,0:T(8,128)}) %all-reduce.9.cloned.1.call-update) | async-done | bytes 262160 | tf_op jit(solution)/shard_map/psum | solution.py:34
  682.5 1.0 copy.15
  683.5 0.2 fusion.8
  683.7 1.3 fusion.4
  685.0 0.0 all-reduce.11.cloned.1.call-update
  685.0 0.0 reduce-scatter.4.cloned.1.call-start
  685.1 111.1 %all-reduce.11.cloned.1.call-done = f32[2,16,1024]{2,1,0:T(8,128)} async-done(((f32[2,16,1024]{2,1,0:T(8,128)}), f32[2,16,1024]{2,1,0:T(8,128)}) %all-reduce.11.cloned.1.call-update) | async-done | bytes 131088 | tf_op jit(solution)/shard_map/psum | solution.py:41
  796.2 0.0 copy-done.2
  796.2 2.0 fusion.2
  798.2 0.1 copy.12
  798.4 0.9 reshape.76
  799.2 0.0 reduce-scatter.4.cloned.1.call-update
  799.3 0.8 constant_dynamic-slice_fusion
  800.0 0.7 copy.9
  800.7 23.3 %reduce-scatter.4.cloned.1.call-done = f32[64,32]{1,0:T(8,128)} async-done(((f32[256,32]{1,0:T(8,128)}), f32[64,32]{1,0:T(8,128)}) %reduce-scatter.4.cloned.1.call-update) | async-done | bytes 8208
  824.1 0.9 reshape.77
  824.9 0.7 copy.13
Async XLA Ops:
  7.2 1.6 copy-start
  7.2 4.9 copy-start.4
  7.2 125.2 %copy-start.1 = (f32[2,128,1024]{2,1,0:T(8,128)S(1)}, f32[2,128,1024]{2,1,0:T(8,128)}, u32[]{:S(2)}) copy-start(f32[2,128,1024]{2,1,0:T(8,128)} %param.8) | copy-start | bytes 3145732
  7.2 402.6 %copy-start.3 = (f32[8,4096]{1,0:T(8,128)S(1)}, f32[8,4096]{1,0:T(8,128)}, u32[]{:S(2)}) copy-start(f32[8,4096]{1,0:T(8,128)} %param.11) | copy-start | bytes 393220
  7.2 125.2 %all-reduce.5.cloned.1.call-start = ((), (), s32[]{:S(2)}) async-start(), calls=%async_computation.1 | async-start | bytes 262144 | tf_op jit(solution)/shard_map/psum | solution.py:24
  12.0 397.8 %all-reduce.7.cloned.1.call-start = ((), (), s32[]{:S(2)}) async-start(), calls=%async_computation.2 | async-start | bytes 524288 | tf_op jit(solution)/shard_map/psum | solution.py:30
  134.7 661.5 %copy-start.2 = (f32[2,16,1024]{2,1,0:T(8,128)S(1)}, f32[2,16,1024]{2,1,0:T(8,128)}, u32[]{:S(2)}) copy-start(f32[2,16,1024]{2,1,0:T(8,128)} %all-reduce.5.cloned.1.call-done) | copy-start | bytes 393220
  135.6 546.9 %all-reduce.9.cloned.1.call-start = ((), (), s32[]{:S(2)}) async-start(), calls=%async_computation.3 | async-start | bytes 524288 | tf_op jit(solution)/shard_map/psum | solution.py:34
  412.4 383.8 %all-reduce.11.cloned.1.call-start = ((), (), s32[]{:S(2)}) async-start(), calls=%async_computation.4 | async-start | bytes 262144 | tf_op jit(solution)/shard_map/psum | solution.py:41
  685.0 139.1 %reduce-scatter.4.cloned.1.call-start = ((), (), s32[]{:S(2)}) async-start(), calls=%async_computation.5 | async-start | bytes 163840
Sparse Core Ops, SparseCore 0:
  12.1 120.2 all-reduce.4
  137.4 272.3 all-reduce.6
  414.8 267.6 all-reduce.8
  685.1 111.0 all-reduce.10
  799.4 24.6 reduce-scatter.3
where the time goes:
time: 834 us; the launch traced here: 832 us
  waiting for transfers between devices  799 us (96%)
  between operations  13.9 us (2%)
  matrix products  11.6 us (1%)
    psum x1, waiting for transfers between devices, body(): total = lax.psum(contrib, ('leaf', 'row', 'col'))  274 us
    psum x1, waiting for transfers between devices, body(): sep_whole = lax.psum(back_terms, ('leaf', 'row', 'col'))  270 us
    psum x1, waiting for transfers between devices, body(): forward = lax.psum(partial_fwd, 'col')  120 us
    psum x1, waiting for transfers between devices, body(): pull_total = lax.psum(pull_terms, 'col')  111 us
    unnamed x6, waiting for transfers between devices  23.4 us
  transfers between devices with their start and end apart: 5, of which 5 were waited for; matrix products, arithmetic and copies ran while one was open for 0% of the time, Pallas kernels for 0%

commit v1 on v0

v1 whole, which is shorter than its diff:
```python
import functools

import jax
import jax.numpy as jnp
from jax import lax
from jax.experimental import pallas as pl
from jax.experimental.pallas import tpu as pltpu
from jax.sharding import PartitionSpec as P

BLOCK = 128
NZ, NX, NC, NY = 8, 4, 16, 8
F32 = jnp.float32
BF16 = jnp.bfloat16
NT = (((1,), (1,)), ((), ()))
NN = (((1,), (0,)), ((), ()))

COL_STEPS = [(dy, dc) for dy in (4, 3, 5, 2, 6, 1, 7, 0) for dc in (0, 1) if (dy, dc) != (0, 0)]
Z_STEPS = (4, 3, 5, 2, 6, 1, 7)
X_STEPS = (2, 1, 3)


def halves(a):
    hi = a.astype(BF16)
    return hi, (a - hi.astype(F32)).astype(BF16)


def dot3(a, b_hi, b_lo, dims):
    m = a.shape[0]
    a_hi, a_lo = halves(a)
    both = lax.dot_general(jnp.concatenate([a_hi, a_lo], axis=0), b_hi, dims, preferred_element_type=F32)
    rest = lax.dot_general(a_hi, b_lo, dims, preferred_element_type=F32)
    return both[:m] + (both[m:] + rest)


def kernel(
    map_ref, rhs_hbm, l_hbm, u_hbm, srhs_hbm, s_hbm, leaf_out, sep_out,
    rhs_v, l_v, u_v, srhs_v, l_hi, l_lo, u_hi, u_lo, s_v, s_hi, s_lo,
    part, a_rs, fwd, xs, b1, b2, b3s, b3, c_ar, d_ar, e1, e2s, e2, fs, f_rs, red, gs, g_rs,
    load_sem, send_sem, recv_sem,
):
    z = lax.axis_index("leaf")
    x = lax.axis_index("row")
    me = lax.axis_index("col")
    y = me // 2
    core = me % 2

    def col_peer(step):
        return lax.rem(y + step[0], NY) * 2 + lax.rem(core + step[1], 2)

    def z_peer(step):
        return lax.rem(z + step, NZ)

    def x_peer(step):
        return lax.rem(x + step, NX)

    barrier = pltpu.get_barrier_semaphore()
    for step in COL_STEPS:
        pl.semaphore_signal(barrier, inc=1, device_id={"col": col_peer(step)}, device_id_type=pl.DeviceIdType.MESH)
    for step in Z_STEPS:
        pl.semaphore_signal(barrier, inc=1, device_id={"leaf": z_peer(step)}, device_id_type=pl.DeviceIdType.MESH)
    for step in X_STEPS:
        pl.semaphore_signal(barrier, inc=1, device_id={"row": x_peer(step)}, device_id_type=pl.DeviceIdType.MESH)

    loads = [
        pltpu.make_async_copy(rhs_hbm, rhs_v, load_sem.at[0]),
        pltpu.make_async_copy(l_hbm.at[0], l_v.at[0], load_sem.at[1]),
        pltpu.make_async_copy(l_hbm.at[1], l_v.at[1], load_sem.at[2]),
        pltpu.make_async_copy(u_hbm, u_v, load_sem.at[3]),
        pltpu.make_async_copy(s_hbm.at[:, pl.ds(pl.multiple_of(z * 512, 512), 512)], s_v.at[x, z], load_sem.at[4]),
        pltpu.make_async_copy(srhs_hbm.at[:, pl.ds(pl.multiple_of(z * 512, 512), 512)], srhs_v, load_sem.at[5]),
    ]
    for copy in loads:
        copy.start()

    def send(stage, src, dst, where):
        pltpu.make_async_remote_copy(
            src_ref=src, dst_ref=dst, send_sem=send_sem.at[stage], recv_sem=recv_sem.at[stage],
            device_id=where, device_id_type=pl.DeviceIdType.MESH,
        ).start()

    def landed(stage, buf, count):
        view = buf.at[pl.ds(0, count)]
        pltpu.make_async_copy(view, view, recv_sem.at[stage]).wait()

    def drained(stage, buf, count):
        view = buf.at[pl.ds(0, count)]
        pltpu.make_async_copy(view, view, send_sem.at[stage]).wait()

    loads[0].wait()
    for s in range(2):
        loads[1 + s].wait()
        hi, lo = halves(l_v[s])
        l_hi[s] = hi
        l_lo[s] = lo
        p = dot3(rhs_v[s], hi, lo, NT)
        for j in range(8):
            part[s * 8 + j] = p[:, j * 128:(j + 1) * 128]

    pl.semaphore_wait(barrier, len(COL_STEPS) + len(Z_STEPS) + len(X_STEPS))
    for step in COL_STEPS:
        peer = col_peer(step)
        send(0, part.at[peer], a_rs.at[me], {"col": peer})
    for step in Z_STEPS:
        peer = z_peer(step)
        send(1, s_hbm.at[:, pl.ds(pl.multiple_of(peer * 512, 512), 512)], s_v.at[x, z], {"leaf": peer})
    a_rs[me] = part[me]
    loads[3].wait()
    for s in range(2):
        hi, lo = halves(u_v[s])
        u_hi[s] = hi
        u_lo[s] = lo
    landed(0, a_rs, 15)
    fwd[me] = jnp.sum(a_rs[...], axis=0)
    for step in COL_STEPS:
        peer = col_peer(step)
        send(2, fwd.at[me], fwd.at[me], {"col": peer})

    loads[4].wait()
    view = s_v.at[0, pl.ds(0, 7)]
    pltpu.make_async_copy(view, view, recv_sem.at[1]).wait()
    for step in X_STEPS:
        send(3, s_v.at[x], s_v.at[x], {"row": x_peer(step)})

    loads[5].wait()
    srhs4 = jnp.zeros((4, 512), F32)
    for k in range(NX):
        srhs4 = srhs4 + jnp.where(x == k, srhs_v[4 * k:4 * k + 4, :], 0.0)
    low = lax.broadcasted_iota(jnp.int32, (8, 128), 0) < 4

    landed(2, fwd, 15)
    coupled = []
    for s in range(2):
        f = jnp.concatenate([fwd[s * 8 + j] for j in range(8)], axis=1)
        coupled.append(dot3(f, u_hi[s], u_lo[s], NT))
    for k in range(NX):
        xs[k] = jnp.concatenate([coupled[0][4 * k:4 * k + 4], coupled[1][4 * k:4 * k + 4]], axis=0)
    for step in X_STEPS:
        peer = x_peer(step)
        send(4, xs.at[peer], b1.at[x], {"row": peer})
    b1[x] = xs[x]
    landed(4, b1, 3)
    b2[me] = jnp.sum(b1[...], axis=0)
    for step in COL_STEPS:
        send(5, b2.at[me], b2.at[me], {"col": col_peer(step)})

    landed(3, s_v, 3)
    for k in range(NX):
        hi, lo = halves(s_v[k].reshape(64, 512))
        s_hi[k * 64:(k + 1) * 64] = hi
        s_lo[k * 64:(k + 1) * 64] = lo
    which = [jnp.where(low, map_ref[0, k], map_ref[1, k]) for k in range(NC)]

    landed(5, b2, 15)
    tiles = [b2[k] for k in range(NC)]
    for b in range(0, 32, 2):
        pair = []
        for block in (b, b + 1):
            acc = jnp.where(which[0] == block, tiles[0], 0.0)
            for k in range(1, NC):
                acc = acc + jnp.where(which[k] == block, tiles[k], 0.0)
            pair.append(acc + pltpu.roll(acc, 4, 0))
        b3s[b // 4, (b // 2) % 2] = jnp.where(low, pair[0], pair[1])
    for step in Z_STEPS:
        peer = z_peer(step)
        send(6, b3s.at[peer], b3.at[z], {"leaf": peer})
    b3[z] = b3s[z]
    landed(6, b3, 7)
    scattered = jnp.sum(b3[...], axis=0)
    updated = srhs4 - jnp.concatenate(
        [scattered[0, 0:4], scattered[0, 4:8], scattered[1, 0:4], scattered[1, 4:8]], axis=1
    )
    sf = dot3(updated, s_hi[...], s_lo[...], NT)
    c_ar[z] = jnp.concatenate([sf[:, :128], sf[:, 128:]], axis=0)
    for step in Z_STEPS:
        send(7, c_ar.at[z], c_ar.at[z], {"leaf": z_peer(step)})
    landed(7, c_ar, 7)
    sf = jnp.sum(c_ar[...], axis=0)
    sf = jnp.concatenate([sf[0:4], sf[4:8]], axis=1)
    back = dot3(sf, s_hi[...], s_lo[...], NN)
    for p in range(2):
        d_ar[me, p] = jnp.concatenate(
            [back[:, p * 256:p * 256 + 128], back[:, p * 256 + 128:p * 256 + 256]], axis=0
        )
    for step in COL_STEPS:
        send(8, d_ar.at[me], d_ar.at[me], {"col": col_peer(step)})
    landed(8, d_ar, 15)
    sol = jnp.sum(d_ar[...], axis=0)
    e1[z] = sol
    for step in Z_STEPS:
        send(9, e1.at[z], e1.at[z], {"leaf": z_peer(step)})
    for k in range(NX):
        half = sol[k // 2, 4 * (k % 2):4 * (k % 2) + 4]
        e2s[k, 1] = jnp.concatenate([half, half], axis=0)
    landed(9, e1, 7)
    picked = []
    for s in range(2):
        target = map_ref[s, me]
        acc = jnp.zeros((8, 128), F32)
        for q in range(16):
            block = jnp.where(low, 2 * q, 2 * q + 1)
            acc = acc + jnp.where(block == target, e1[q // 2, q % 2], 0.0)
        picked.append(acc + pltpu.roll(acc, 4, 0))
    pulled_tile = jnp.where(low, picked[0], picked[1])
    for k in range(NX):
        e2s[k, 0] = pulled_tile
    for step in X_STEPS:
        peer = x_peer(step)
        send(10, e2s.at[peer], e2.at[x], {"row": peer})
    e2[x] = e2s[x]
    landed(10, e2, 3)
    for s in range(2):
        pulled = jnp.concatenate([e2[k, 0, 4 * s:4 * s + 4] for k in range(NX)], axis=0)
        p = dot3(pulled, u_hi[s], u_lo[s], NN)
        for j in range(8):
            fs[s * 8 + j] = p[:, j * 128:(j + 1) * 128]
    for step in COL_STEPS:
        peer = col_peer(step)
        send(11, fs.at[peer], f_rs.at[me], {"col": peer})
    f_rs[me] = fs[me]
    block = jnp.concatenate([e2[k, 1, 0:4] for k in range(NX)], axis=0)
    sep_out[...] = pltpu.roll(block, lax.rem(128 - 8 * me, 128), 1)[:, :8]
    landed(11, f_rs, 15)
    red[me] = fwd[me] - jnp.sum(f_rs[...], axis=0)
    for step in COL_STEPS:
        send(12, red.at[me], red.at[me], {"col": col_peer(step)})
    landed(12, red, 15)
    lp = []
    for s in range(2):
        f = jnp.concatenate([red[s * 8 + j] for j in range(8)], axis=1)
        lp.append(dot3(f, l_hi[s], l_lo[s], NN))
    for k in range(NX):
        gs[k] = jnp.concatenate([lp[0][:, k * 64:(k + 1) * 64], lp[1][:, k * 64:(k + 1) * 64]], axis=1)
    for step in X_STEPS:
        peer = x_peer(step)
        send(13, gs.at[peer], g_rs.at[x], {"row": peer})
    g_rs[x] = gs[x]
    drained(0, part, 15)
    view = s_v.at[0, pl.ds(0, 7)]
    pltpu.make_async_copy(view, view, send_sem.at[1]).wait()
    drained(2, fwd, 15)
    drained(3, s_v, 3)
    drained(4, xs, 3)
    drained(5, b2, 15)
    drained(6, b3s, 7)
    drained(7, c_ar, 7)
    drained(8, d_ar, 15)
    drained(9, e1, 7)
    drained(10, e2s, 3)
    drained(11, fs, 15)
    drained(12, red, 15)
    landed(13, g_rs, 3)
    total = jnp.sum(g_rs[...], axis=0)
    leaf_out[0] = total[:, :64]
    leaf_out[1] = total[:, 64:]
    drained(13, gs, 3)


def body(leaf_rhs, leaf_inverse, update_rows, update_map, sep_rhs, sep_inverse):
    hbm = pl.BlockSpec(memory_space=pl.ANY)
    vmem = pl.BlockSpec(memory_space=pltpu.VMEM)
    stages = 14
    return pl.pallas_call(
        kernel,
        name="substitution",
        out_shape=(jax.ShapeDtypeStruct((2, 16, 64), F32), jax.ShapeDtypeStruct((16, 8), F32)),
        in_specs=[pl.BlockSpec(memory_space=pltpu.SMEM), hbm, hbm, hbm, hbm, hbm],
        out_specs=(vmem, vmem),
        scratch_shapes=[
            pltpu.VMEM((2, 16, 256), F32),
            pltpu.VMEM((2, 1024, 256), F32),
            pltpu.VMEM((2, 128, 1024), F32),
            pltpu.VMEM((16, 512), F32),
            pltpu.VMEM((2, 1024, 256), BF16),
            pltpu.VMEM((2, 1024, 256), BF16),
            pltpu.VMEM((2, 128, 1024), BF16),
            pltpu.VMEM((2, 128, 1024), BF16),
            pltpu.VMEM((NX, NZ, 8, 512), F32),
            pltpu.VMEM((256, 512), BF16),
            pltpu.VMEM((256, 512), BF16),
            pltpu.VMEM((NC, 16, 128), F32),
            pltpu.VMEM((NC, 16, 128), F32),
            pltpu.VMEM((NC, 16, 128), F32),
            pltpu.VMEM((NX, 8, 128), F32),
            pltpu.VMEM((NX, 8, 128), F32),
            pltpu.VMEM((NC, 8, 128), F32),
            pltpu.VMEM((NZ, 2, 8, 128), F32),
            pltpu.VMEM((NZ, 2, 8, 128), F32),
            pltpu.VMEM((NZ, 8, 128), F32),
            pltpu.VMEM((NC, 2, 8, 128), F32),
            pltpu.VMEM((NZ, 2, 8, 128), F32),
            pltpu.VMEM((NX, 2, 8, 128), F32),
            pltpu.VMEM((NX, 2, 8, 128), F32),
            pltpu.VMEM((NC, 16, 128), F32),
            pltpu.VMEM((NC, 16, 128), F32),
            pltpu.VMEM((NC, 16, 128), F32),
            pltpu.VMEM((NX, 16, 128), F32),
            pltpu.VMEM((NX, 16, 128), F32),
            pltpu.SemaphoreType.DMA((6,)),
            pltpu.SemaphoreType.DMA((stages,)),
            pltpu.SemaphoreType.DMA((stages,)),
        ],
        compiler_params=pltpu.CompilerParams(collective_id=0, has_side_effects=True),
    )(update_map, leaf_rhs, leaf_inverse, update_rows, sep_rhs, sep_inverse)


def solution(mesh):
    in_specs = (
        P("leaf", None, "col"),
        P("leaf", "row", "col"),
        P("leaf", "col", "row"),
        P("leaf", None),
        P(),
        P(("leaf", "row", "col"), None),
    )
    out_specs = (P("leaf", None, ("col", "row")), P(None, ("leaf", "row", "col")))
    return jax.shard_map(body, mesh=mesh, in_specs=in_specs, out_specs=out_specs, check_vma=False)
```

time: 834 us -> 76.6 us (0.09)
  waiting for transfers between devices: 799 us -> 0 us
  Pallas kernels: 0 us -> 73 us
  between operations: 13.9 us -> 0.64 us
  matrix products: 11.6 us -> 0 us
    psum x4 -> x0, waiting for transfers between devices: 775 us -> none  [the longest x1 274 us: body(): total = lax.psum(contrib, ('leaf', 'row', 'col'))]
    pallas_call x0 -> x1, Pallas kernels: none -> 73 us  [body(): pl.pallas_call(kernel, name='substitution', out_shape=(jax.ShapeDtypeStru...]
    unnamed x6 -> x0, waiting for transfers between devices: 23.4 us -> none
    dot_general x8 -> x0, matrix products: 11.6 us -> none  [the longest x1 3.23 us: body(): jnp.einsum('sij,srj->sri', leaf_inverse, leaf_rhs, precision=HIGH)]
  transfers between devices with their start and end apart: 5 -> 0, of which waited for: 5 -> 0; matrix products, arithmetic and copies ran while one was open for 0% -> 0% of each run, Pallas kernels for 0% -> 0%
where the time goes in v1:
time: 76.6 us; the launch traced here: 76.3 us
  Pallas kernels  73 us (95%)
  local copies, waits for them, and re-layouts  2.68 us (3%)
    pallas_call x1, Pallas kernels, body(): pl.pallas_call(kernel, name='substitution', out_shape=(jax.ShapeDtypeStru...  73 us

profile of v1, /device:TPU:1, one launch (start us, length us, event | category | flops | bytes accessed | tf_op | source)
XLA Modules:
  0.0 76.3 jit_solution(10397612738673609774)
XLA Ops:
  0.6 73.0 %substitution.1 = (f32[2,16,64]{2,1,0:T(8,128)}, f32[16,8]{1,0:T(8,128)}) custom-call(s32[2,16]{1,0:T(2,128)} %map_ref.1, f32[2,16,256]{2,1,0:T(8,128)} %rhs_hbm.1, f32[2,1024,256]{2,1,0:T(8,128)} %l_hbm.1, f32[2,128,1024]{2,1,0:T(8,128)} %u_hbm.1, f32[16,4096]{1,0:T(8,128)} %srhs_hbm.1, f32[8,4096]{1,0:T(8,128)} %s_hbm.1), custom_call_target="tpu_custom_call" | custom-call | tf_op jit(solution)/shard_map/substitution/pallas_call | solution.py:262
  73.6 1.4 %copy.8 = f32[16,8]{0,1:T(8,128)} copy(f32[16,8]{1,0:T(8,128)} %get-tuple-element.3) | data formatting | bytes 1024 | tf_op jit(solution)/shard_map/substitution/pallas_call | solution.py:262
  75.0 1.3 %copy.10 = f32[2,16,64]{2,1,0:T(8,128)} copy(f32[2,16,64]{2,1,0:T(8,128)} %get-tuple-element.6) | data formatting | bytes 16384

commit v2 on v1

--- a/solution.py
+++ b/solution.py
@@ -33,8 +33,8 @@
 
 
 def kernel(
-    map_ref, rhs_hbm, l_hbm, u_hbm, srhs_hbm, s_hbm, leaf_out, sep_out,
-    rhs_v, l_v, u_v, srhs_v, l_hi, l_lo, u_hi, u_lo, s_v, s_hi, s_lo,
+    map_hbm, rhs_hbm, l_hbm, u_hbm, srhs_hbm, s_hbm, leaf_out, sep_out,
+    map_ref, rhs_v, l_v, u_v, srhs_v, l_hi, l_lo, u_hi, u_lo, s_v, s_hi, s_lo,
     part, a_rs, fwd, xs, b1, b2, b3s, b3, c_ar, d_ar, e1, e2s, e2, fs, f_rs, red, gs, g_rs,
     load_sem, send_sem, recv_sem,
 ):
@@ -53,24 +53,30 @@
     def x_peer(step):
         return lax.rem(x + step, NX)
 
-    barrier = pltpu.get_barrier_semaphore()
-    for step in COL_STEPS:
-        pl.semaphore_signal(barrier, inc=1, device_id={"col": col_peer(step)}, device_id_type=pl.DeviceIdType.MESH)
-    for step in Z_STEPS:
-        pl.semaphore_signal(barrier, inc=1, device_id={"leaf": z_peer(step)}, device_id_type=pl.DeviceIdType.MESH)
-    for step in X_STEPS:
-        pl.semaphore_signal(barrier, inc=1, device_id={"row": x_peer(step)}, device_id_type=pl.DeviceIdType.MESH)
-
     loads = [
         pltpu.make_async_copy(rhs_hbm, rhs_v, load_sem.at[0]),
-        pltpu.make_async_copy(l_hbm.at[0], l_v.at[0], load_sem.at[1]),
-        pltpu.make_async_copy(l_hbm.at[1], l_v.at[1], load_sem.at[2]),
-        pltpu.make_async_copy(u_hbm, u_v, load_sem.at[3]),
-        pltpu.make_async_copy(s_hbm.at[:, pl.ds(pl.multiple_of(z * 512, 512), 512)], s_v.at[x, z], load_sem.at[4]),
-        pltpu.make_async_copy(srhs_hbm.at[:, pl.ds(pl.multiple_of(z * 512, 512), 512)], srhs_v, load_sem.at[5]),
+        *(
+            pltpu.make_async_copy(
+                l_hbm.at[s, pl.ds(h * 512, 512)], l_v.at[s, pl.ds(h * 512, 512)], load_sem.at[1 + 2 * s + h]
+            )
+            for s in range(2)
+            for h in range(2)
+        ),
+        pltpu.make_async_copy(u_hbm, u_v, load_sem.at[5]),
+        pltpu.make_async_copy(s_hbm.at[:, pl.ds(pl.multiple_of(z * 512, 512), 512)], s_v.at[x, z], load_sem.at[6]),
+        pltpu.make_async_copy(srhs_hbm.at[:, pl.ds(pl.multiple_of(z * 512, 512), 512)], srhs_v, load_sem.at[7]),
+        pltpu.make_async_copy(map_hbm, map_ref, load_sem.at[8]),
     ]
     for copy in loads:
         copy.start()
+
+    barrier = pltpu.get_barrier_semaphore()
+    for step in COL_STEPS:
+        pl.semaphore_signal(barrier, inc=1, device_id={"col": col_peer(step)}, device_id_type=pl.DeviceIdType.MESH)
+    for step in Z_STEPS:
+        pl.semaphore_signal(barrier, inc=1, device_id={"leaf": z_peer(step)}, device_id_type=pl.DeviceIdType.MESH)
+    for step in X_STEPS:
+        pl.semaphore_signal(barrier, inc=1, device_id={"row": x_peer(step)}, device_id_type=pl.DeviceIdType.MESH)
 
     def send(stage, src, dst, where):
         pltpu.make_async_remote_copy(
@@ -88,13 +94,15 @@
 
     loads[0].wait()
     for s in range(2):
-        loads[1 + s].wait()
-        hi, lo = halves(l_v[s])
-        l_hi[s] = hi
-        l_lo[s] = lo
-        p = dot3(rhs_v[s], hi, lo, NT)
-        for j in range(8):
-            part[s * 8 + j] = p[:, j * 128:(j + 1) * 128]
+        for h in range(2):
+            loads[1 + 2 * s + h].wait()
+            rows = pl.ds(h * 512, 512)
+            hi, lo = halves(l_v[s, rows])
+            l_hi[s, rows] = hi
+            l_lo[s, rows] = lo
+            p = dot3(rhs_v[s], hi, lo, NT)
+            for j in range(4):
+                part[2 * (4 * h + j) + s] = p[:, j * 128:(j + 1) * 128]
 
     pl.semaphore_wait(barrier, len(COL_STEPS) + len(Z_STEPS) + len(X_STEPS))
     for step in COL_STEPS:
@@ -104,7 +112,7 @@
         peer = z_peer(step)
         send(1, s_hbm.at[:, pl.ds(pl.multiple_of(peer * 512, 512), 512)], s_v.at[x, z], {"leaf": peer})
     a_rs[me] = part[me]
-    loads[3].wait()
+    loads[5].wait()
     for s in range(2):
         hi, lo = halves(u_v[s])
         u_hi[s] = hi
@@ -115,13 +123,14 @@
         peer = col_peer(step)
         send(2, fwd.at[me], fwd.at[me], {"col": peer})
 
-    loads[4].wait()
+    loads[6].wait()
     view = s_v.at[0, pl.ds(0, 7)]
     pltpu.make_async_copy(view, view, recv_sem.at[1]).wait()
     for step in X_STEPS:
         send(3, s_v.at[x], s_v.at[x], {"row": x_peer(step)})
 
-    loads[5].wait()
+    loads[7].wait()
+    loads[8].wait()
     srhs4 = jnp.zeros((4, 512), F32)
     for k in range(NX):
         srhs4 = srhs4 + jnp.where(x == k, srhs_v[4 * k:4 * k + 4, :], 0.0)
@@ -130,7 +139,7 @@
     landed(2, fwd, 15)
     coupled = []
     for s in range(2):
-        f = jnp.concatenate([fwd[s * 8 + j] for j in range(8)], axis=1)
+        f = jnp.concatenate([fwd[2 * j + s] for j in range(8)], axis=1)
         coupled.append(dot3(f, u_hi[s], u_lo[s], NT))
     for k in range(NX):
         xs[k] = jnp.concatenate([coupled[0][4 * k:4 * k + 4], coupled[1][4 * k:4 * k + 4]], axis=0)
@@ -212,13 +221,13 @@
         pulled = jnp.concatenate([e2[k, 0, 4 * s:4 * s + 4] for k in range(NX)], axis=0)
         p = dot3(pulled, u_hi[s], u_lo[s], NN)
         for j in range(8):
-            fs[s * 8 + j] = p[:, j * 128:(j + 1) * 128]
+            fs[2 * j + s] = p[:, j * 128:(j + 1) * 128]
     for step in COL_STEPS:
         peer = col_peer(step)
         send(11, fs.at[peer], f_rs.at[me], {"col": peer})
     f_rs[me] = fs[me]
     block = jnp.concatenate([e2[k, 1, 0:4] for k in range(NX)], axis=0)
-    sep_out[...] = pltpu.roll(block, lax.rem(128 - 8 * me, 128), 1)[:, :8]
+    sep_out[...] = jnp.transpose(pltpu.roll(block, lax.rem(128 - 8 * me, 128), 1))[:8]
     landed(11, f_rs, 15)
     red[me] = fwd[me] - jnp.sum(f_rs[...], axis=0)
     for step in COL_STEPS:
@@ -226,7 +235,7 @@
     landed(12, red, 15)
     lp = []
     for s in range(2):
-        f = jnp.concatenate([red[s * 8 + j] for j in range(8)], axis=1)
+        f = jnp.concatenate([red[2 * j + s] for j in range(8)], axis=1)
         lp.append(dot3(f, l_hi[s], l_lo[s], NN))
     for k in range(NX):
         gs[k] = jnp.concatenate([lp[0][:, k * 64:(k + 1) * 64], lp[1][:, k * 64:(k + 1) * 64]], axis=1)
@@ -255,17 +264,23 @@
     drained(13, gs, 3)
 
 
+def finish(leaf_in, sep_in, leaf_out, sep_out):
+    leaf_out[...] = leaf_in[...]
+    sep_out[...] = sep_in[...]
+
+
 def body(leaf_rhs, leaf_inverse, update_rows, update_map, sep_rhs, sep_inverse):
     hbm = pl.BlockSpec(memory_space=pl.ANY)
     vmem = pl.BlockSpec(memory_space=pltpu.VMEM)
     stages = 14
-    return pl.pallas_call(
+    leaf, sep = pl.pallas_call(
         kernel,
         name="substitution",
-        out_shape=(jax.ShapeDtypeStruct((2, 16, 64), F32), jax.ShapeDtypeStruct((16, 8), F32)),
-        in_specs=[pl.BlockSpec(memory_space=pltpu.SMEM), hbm, hbm, hbm, hbm, hbm],
+        out_shape=(pltpu.VMEM((2, 16, 64), F32), pltpu.VMEM((8, 16), F32)),
+        in_specs=[hbm, hbm, hbm, hbm, hbm, hbm],
         out_specs=(vmem, vmem),
         scratch_shapes=[
+            pltpu.SMEM((2, 16), jnp.int32),
             pltpu.VMEM((2, 16, 256), F32),
             pltpu.VMEM((2, 1024, 256), F32),
             pltpu.VMEM((2, 128, 1024), F32),
@@ -295,12 +310,20 @@
             pltpu.VMEM((NC, 16, 128), F32),
             pltpu.VMEM((NX, 16, 128), F32),
             pltpu.VMEM((NX, 16, 128), F32),
-            pltpu.SemaphoreType.DMA((6,)),
+            pltpu.SemaphoreType.DMA((9,)),
             pltpu.SemaphoreType.DMA((stages,)),
             pltpu.SemaphoreType.DMA((stages,)),
         ],
         compiler_params=pltpu.CompilerParams(collective_id=0, has_side_effects=True),
     )(update_map, leaf_rhs, leaf_inverse, update_rows, sep_rhs, sep_inverse)
+    leaf, sep = pl.pallas_call(
+        finish,
+        name="finish",
+        out_shape=(jax.ShapeDtypeStruct((2, 16, 64), F32), jax.ShapeDtypeStruct((8, 16), F32)),
+        in_specs=[vmem, vmem],
+        out_specs=(vmem, vmem),
+    )(pltpu.with_memory_space_constraint(leaf, pltpu.VMEM), pltpu.with_memory_space_constraint(sep, pltpu.VMEM))
+    return leaf, sep.T
 
 
 def solution(mesh):

time: 76.6 us -> 72.8 us (0.950)
  local copies, waits for them, and re-layouts: 2.68 us -> 0 us
  Pallas kernels: 73 us -> 72 us
    pallas_call x1 -> x0, local copies, waits for them, and re-layouts: 1.36 us -> none  [body(): pl.pallas_call(kernel, name='substitution', out_shape=(jax.ShapeDtypeStru...]
    unnamed x1 -> x0, local copies, waits for them, and re-layouts: 1.32 us -> none
    pallas_call x1 -> x2, Pallas kernels: 73 us -> 72 us  [the longest x1 71.4 us: body(): pl.pallas_call(kernel, name='substitution', out_shape=(pltpu.VMEM((2, 16,...]
where the time goes in v2:
time: 72.8 us; the launch traced here: 72.7 us
  Pallas kernels  72 us (99%)
    pallas_call x1, Pallas kernels, body(): pl.pallas_call(kernel, name='substitution', out_shape=(pltpu.VMEM((2, 16,...  71.4 us

profile of v2, /device:TPU:1, one launch (start us, length us, event | category | flops | bytes accessed | tf_op | source)
XLA Modules:
  0.0 72.7 jit_solution(4991603604970354736)
XLA Ops:
  0.6 71.4 %substitution.1 = (f32[2,16,64]{2,1,0:T(8,128)S(1)}, f32[8,16]{1,0:T(8,128)S(1)}) custom-call(s32[2,16]{1,0:T(2,128)} %map_hbm.1, f32[2,16,256]{2,1,0:T(8,128)} %rhs_hbm.1, f32[2,1024,256]{2,1,0:T(8,128)} %l_hbm.1, f32[2,128,1024]{2,1,0:T(8,128)} %u_hbm.1, f32[16,4096]{1,0:T(8,128)} %srhs_hbm.1, f32[8,4096]{1,0:T(8,128)} %s_hbm.1), custom_call_target="tpu_custom_call" | custom-call | tf_op jit(solution)/shard_map/substitution/pallas_call | solution.py:276
  72.1 0.6 finish.1

commit v3 on v0

v3 whole, which is shorter than its diff:
```python
import jax
import jax.numpy as jnp
from jax import lax
from jax.experimental import pallas as pl
from jax.experimental.pallas import tpu as pltpu
from jax.sharding import PartitionSpec as P

NZ, NX, NC, NY = 8, 4, 16, 8
F32 = jnp.float32
BF16 = jnp.bfloat16
NT = (((1,), (1,)), ((), ()))
NN = (((1,), (0,)), ((), ()))

Y_STEPS = (4, 3, 5, 2, 6, 1, 7)
COL_STEPS = [(dy, dc) for dy in Y_STEPS + (0,) for dc in (0, 1) if (dy, dc) != (0, 0)]
Z_STEPS = (4, 3, 5, 2, 6, 1, 7)
X_STEPS = (2, 1, 3)
MESH = pl.DeviceIdType.MESH

(A_SUM, S_NEAR, A_GATHER, S_FAR, C_SUM, C_GATHER, S_SWAP, Z_SUM, D_SUM, U_SWAP, D_ROW, F_SUM, F_GATHER, G_SUM,
 L_SWAP, H_ROW, H_COL) = range(17)


def halves(a):
    hi = a.astype(BF16)
    return hi, (a - hi.astype(F32)).astype(BF16)


def dot3(a, b_hi, b_lo, dims):
    m = a.shape[0]
    a_hi, a_lo = halves(a)
    both = lax.dot_general(jnp.concatenate([a_hi, a_lo], axis=0), b_hi, dims, preferred_element_type=F32)
    rest = lax.dot_general(a_hi, b_lo, dims, preferred_element_type=F32)
    return both[:m] + (both[m:] + rest)


def kernel(
    map_hbm, rhs_hbm, l_hbm, u_hbm, srhs_hbm, s_hbm, leaf_out, sep_out,
    map_ref, rhs_v, l_v, l_par, u_own, u_par, srhs_v, l_hi, l_lo, lp_hi, lp_lo, u_hi, u_lo, s_v, s_hi, s_lo,
    part, a_rs, fwd, b1, b2s, b2, c_ar, bs, d_rs, e2, fs, f_rs, red, gs, g_rs, hs, h1, h2,
    load_sem, send_sem, recv_sem,
):
    z = lax.axis_index("leaf")
    x = lax.axis_index("row")
    me = lax.axis_index("col")
    y = me // 2
    core = me % 2
    other = 1 - core
    partner = 2 * y + other

    def col_peer(step):
        return lax.rem(y + step[0], NY) * 2 + lax.rem(core + step[1], 2)

    def y_peer(step):
        return lax.rem(y + step, NY)

    def z_peer(step):
        return lax.rem(z + step, NZ)

    def x_peer(step):
        return lax.rem(x + step, NX)

    s_here = pl.ds(pl.multiple_of(z * 512, 512), 512)
    loads = [
        pltpu.make_async_copy(rhs_hbm, rhs_v, load_sem.at[0]),
        *(
            pltpu.make_async_copy(
                l_hbm.at[s, pl.ds(h * 512, 512)], l_v.at[s, pl.ds(h * 512, 512)], load_sem.at[1 + 2 * s + h]
            )
            for s in range(2)
            for h in range(2)
        ),
        pltpu.make_async_copy(u_hbm.at[core], u_own, load_sem.at[5]),
        pltpu.make_async_copy(s_hbm, s_v.at[core, z], load_sem.at[6]),
        pltpu.make_async_copy(srhs_hbm.at[pl.ds(pl.multiple_of(core * 8, 8), 8), s_here], srhs_v, load_sem.at[7]),
        pltpu.make_async_copy(map_hbm, map_ref, load_sem.at[8]),
    ]
    for copy in loads:
        copy.start()

    barrier = pltpu.get_barrier_semaphore()
    peers = [{"col": col_peer(step)} for step in COL_STEPS]
    peers += [{"leaf": z_peer(step)} for step in Z_STEPS]
    peers += [{"row": x_peer(step)} for step in X_STEPS]
    peers += [{"row": x_peer(step), "col": partner} for step in X_STEPS]
    for peer in peers:
        pl.semaphore_signal(barrier, inc=1, device_id=peer, device_id_type=MESH)

    def send(stage, src, dst, where):
        pltpu.make_async_remote_copy(
            src_ref=src, dst_ref=dst, send_sem=send_sem.at[stage], recv_sem=recv_sem.at[stage],
            device_id=where, device_id_type=MESH,
        ).start()

    def landed(stage, view):
        pltpu.make_async_copy(view, view, recv_sem.at[stage]).wait()

    def drained(stage, view):
        pltpu.make_async_copy(view, view, send_sem.at[stage]).wait()

    loads[0].wait()
    for s in range(2):
        for h in range(2):
            loads[1 + 2 * s + h].wait()
            rows = pl.ds(h * 512, 512)
            hi, lo = halves(l_v[s, rows])
            l_hi[s, rows] = hi
            l_lo[s, rows] = lo
            p = dot3(rhs_v[s], hi, lo, NT)
            for j in range(4):
                part[2 * (4 * h + j) + s] = p[:, j * 128:(j + 1) * 128]

    pl.semaphore_wait(barrier, len(peers))
    for step in COL_STEPS:
        peer = col_peer(step)
        send(A_SUM, part.at[peer], a_rs.at[me], {"col": peer})
    send(U_SWAP, u_hbm.at[other], u_par, {"col": partner})
    for step in (1, 7, 2, 6):
        send(S_NEAR, s_hbm, s_v.at[core, z], {"leaf": z_peer(step)})
    send(S_SWAP, s_hbm, s_v.at[core, z], {"col": partner})
    a_rs[me] = part[me]
    loads[5].wait()
    hi, lo = halves(u_own[...])
    u_hi[0:128] = hi
    u_lo[0:128] = lo
    landed(U_SWAP, u_par)
    hi, lo = halves(u_par[...])
    u_hi[128:256] = hi
    u_lo[128:256] = lo

    landed(A_SUM, a_rs.at[pl.ds(0, 15)])
    fwd[y] = jnp.sum(a_rs[...], axis=0)
    for step in Y_STEPS:
        send(A_GATHER, fwd.at[y], fwd.at[y], {"col": 2 * y_peer(step) + core})
    send(L_SWAP, l_hbm.at[other], l_par, {"col": partner})
    loads[6].wait()
    loads[7].wait()
    loads[8].wait()

    landed(A_GATHER, fwd.at[pl.ds(0, 7)])
    f = jnp.concatenate([fwd[j] for j in range(8)], axis=1)
    coupled = dot3(f, u_hi[...], u_lo[...], NT)
    for q in range(2):
        b1[x, q] = coupled[:, q * 128:(q + 1) * 128]
    for step in X_STEPS:
        send(C_SUM, b1.at[x], b1.at[x], {"row": x_peer(step)})

    landed(S_NEAR, s_v.at[0, pl.ds(0, 4)])
    below = z_peer(6)
    above = z_peer(2)
    send(S_FAR, s_v.at[core, below], s_v.at[core, below], {"leaf": z_peer(1)})
    send(S_FAR, s_v.at[core, above], s_v.at[core, above], {"leaf": z_peer(7)})
    left = pl.ds(0, 2048)
    right = pl.ds(2048, 2048)
    send(S_FAR, s_v.at[core, below, :, left], s_v.at[core, below, :, left], {"leaf": z_peer(2)})
    send(S_FAR, s_v.at[core, above, :, right], s_v.at[core, above, :, right], {"leaf": z_peer(6)})
    for step in (1, 7, 2, 6):
        where = z_peer(step)
        send(S_SWAP, s_v.at[core, where], s_v.at[core, where], {"col": partner})

    landed(C_SUM, b1.at[pl.ds(0, 3)])
    total = jnp.sum(b1[...], axis=0)
    for h in range(2):
        for q in range(2):
            b2s[h, q] = total[q, 8 * h:8 * h + 8]
    for step in COL_STEPS:
        peer = col_peer(step)
        send(C_GATHER, b2s.at[lax.rem(core + step[1], 2)], b2.at[me], {"col": peer})
    b2[me] = b2s[core]

    landed(S_FAR, s_v.at[0, pl.ds(0, 3)])
    for step in (3, 5, 4):
        where = z_peer(step)
        send(S_SWAP, s_v.at[core, where], s_v.at[core, where], {"col": partner})
    landed(S_SWAP, s_v.at[0])
    for b in range(32):
        hi, lo = halves(s_v[:, :, :, b * 128:(b + 1) * 128].reshape(128, 128))
        s_hi[b] = hi
        s_lo[b] = lo

    def block_pair(k):
        c = k % 2
        return map_ref[c, k], map_ref[c, k + 1 - 2 * c]

    def s_pair(ref, pair):
        return jnp.concatenate([ref[pair[0]], ref[pair[1]]], axis=1)

    acc = jnp.zeros((8, 128), F32)
    for i in range(2):
        pair = (4 * z + 2 * i, 4 * z + 2 * i + 1)
        acc = acc + dot3(srhs_v[:, i * 256:(i + 1) * 256], s_pair(s_hi, pair), s_pair(s_lo, pair), NT)

    landed(C_GATHER, b2.at[pl.ds(0, 15)])
    for k in range(NC):
        pair = block_pair(k)
        raw = jnp.concatenate([b2[k, 0], b2[k, 1]], axis=1)
        acc = acc - dot3(raw, s_pair(s_hi, pair), s_pair(s_lo, pair), NT)
    c_ar[z] = acc
    for step in Z_STEPS:
        send(Z_SUM, c_ar.at[z], c_ar.at[z], {"leaf": z_peer(step)})
    landed(L_SWAP, l_par)
    hi, lo = halves(l_par[...])
    lp_hi[...] = hi
    lp_lo[...] = lo
    landed(Z_SUM, c_ar.at[pl.ds(0, 7)])
    sf = jnp.sum(c_ar[...], axis=0)

    for k in range(NC):
        pair = block_pair(k)
        p = dot3(sf, s_pair(s_hi, pair), s_pair(s_lo, pair), NN)
        bs[k, 0] = p[:, :128]
        bs[k, 1] = p[:, 128:]
    for step in COL_STEPS:
        peer = col_peer(step)
        send(D_SUM, bs.at[peer], d_rs.at[me], {"col": peer})
    d_rs[me] = bs[me]
    for i in range(2):
        pair = (4 * z + 2 * i, 4 * z + 2 * i + 1)
        p = dot3(sf, s_pair(s_hi, pair), s_pair(s_lo, pair), NN)
        hs[2 * i] = p[:, :128]
        hs[2 * i + 1] = p[:, 128:]
    for step in X_STEPS:
        peer = x_peer(step)
        send(H_ROW, hs.at[peer], h1.at[x], {"row": peer})
    h1[x] = hs[x]
    landed(H_ROW, h1.at[pl.ds(0, 3)])
    h2[me] = jnp.sum(h1[...], axis=0)

    landed(D_SUM, d_rs.at[pl.ds(0, 15)])
    for h in range(2):
        half = d_rs[h]
        for k in range(1, NY):
            half = half + d_rs[2 * k + h]
        for q in range(2):
            e2[x, q, 8 * h:8 * h + 8] = half[q]
    for step in X_STEPS:
        send(D_ROW, e2.at[x], e2.at[x], {"row": x_peer(step)})
    for step in COL_STEPS:
        send(H_COL, h2.at[me], h2.at[me], {"col": col_peer(step)})
    landed(D_ROW, e2.at[pl.ds(0, 3)])
    pulled = jnp.sum(e2[...], axis=0)
    p = dot3(jnp.concatenate([pulled[0], pulled[1]], axis=1), u_hi[...], u_lo[...], NN)
    for j in range(8):
        fs[j] = p[:, j * 128:(j + 1) * 128]
    for step in Y_STEPS:
        peer = y_peer(step)
        send(F_SUM, fs.at[peer], f_rs.at[y], {"col": 2 * peer + core})
    f_rs[y] = fs[y]
    landed(H_COL, h2.at[pl.ds(0, 15)])
    block = []
    for h in range(2):
        half = h2[h]
        for k in range(1, NY):
            half = half + h2[2 * k + h]
        block.append(half)
    block = jnp.concatenate(block, axis=0)
    sep_out[...] = jnp.transpose(pltpu.roll(block, lax.rem(128 - 8 * me, 128), 1))[:8]
    landed(F_SUM, f_rs.at[pl.ds(0, 7)])
    red[y] = fwd[y] - jnp.sum(f_rs[...], axis=0)
    for step in Y_STEPS:
        send(F_GATHER, red.at[y], red.at[y], {"col": 2 * y_peer(step) + core})
    landed(F_GATHER, red.at[pl.ds(0, 7)])
    f = jnp.concatenate([red[j] for j in range(8)], axis=1)
    for where, mine in ((other, False), (core, True)):
        p = dot3(f, l_hi[core], l_lo[core], NN) if mine else dot3(f, lp_hi[...], lp_lo[...], NN)
        for k in range(NX):
            piece = p[:, k * 64:(k + 1) * 64]
            gs[k, where] = jnp.concatenate([piece[:8], piece[8:]], axis=1)
        for step in X_STEPS:
            peer = x_peer(step)
            send(G_SUM, gs.at[peer, where], g_rs.at[x, core], {"row": peer} if mine else {"row": peer, "col": partner})
    send(G_SUM, gs.at[x, other], g_rs.at[x, core], {"col": partner})
    g_rs[x, core] = gs[x, core]
    drained(A_SUM, part.at[pl.ds(0, 15)])
    drained(S_NEAR, s_v.at[0, pl.ds(0, 4)])
    drained(A_GATHER, fwd.at[pl.ds(0, 7)])
    drained(S_FAR, s_v.at[0, pl.ds(0, 3)])
    drained(C_SUM, b1.at[pl.ds(0, 3)])
    drained(C_GATHER, b2.at[pl.ds(0, 15)])
    drained(S_SWAP, s_v.at[0])
    drained(Z_SUM, c_ar.at[pl.ds(0, 7)])
    drained(D_SUM, d_rs.at[pl.ds(0, 15)])
    drained(U_SWAP, u_par)
    drained(D_ROW, e2.at[pl.ds(0, 3)])
    drained(F_SUM, fs.at[pl.ds(0, 7)])
    drained(F_GATHER, red.at[pl.ds(0, 7)])
    drained(L_SWAP, l_par)
    drained(H_ROW, h1.at[pl.ds(0, 3)])
    drained(H_COL, h2.at[pl.ds(0, 15)])
    landed(G_SUM, c_ar.at[pl.ds(0, 7)])
    total = jnp.sum(g_rs[...], axis=0)
    for s in range(2):
        leaf_out[s, 0:8] = total[s][:, :64]
        leaf_out[s, 8:16] = total[s][:, 64:]
    drained(G_SUM, c_ar.at[pl.ds(0, 7)])


def finish(leaf_in, sep_in, leaf_out, sep_out):
    leaf_out[...] = leaf_in[...]
    sep_out[...] = sep_in[...]


def body(leaf_rhs, leaf_inverse, update_rows, update_map, sep_rhs, sep_inverse):
    hbm = pl.BlockSpec(memory_space=pl.ANY)
    vmem = pl.BlockSpec(memory_space=pltpu.VMEM)
    stages = 17
    leaf, sep = pl.pallas_call(
        kernel,
        name="substitution",
        out_shape=(pltpu.VMEM((2, 16, 64), F32), pltpu.VMEM((8, 16), F32)),
        in_specs=[hbm, hbm, hbm, hbm, hbm, hbm],
        out_specs=(vmem, vmem),
        scratch_shapes=[
            pltpu.SMEM((2, 16), jnp.int32),
            pltpu.VMEM((2, 16, 256), F32),
            pltpu.VMEM((2, 1024, 256), F32),
            pltpu.VMEM((1024, 256), F32),
            pltpu.VMEM((128, 1024), F32),
            pltpu.VMEM((128, 1024), F32),
            pltpu.VMEM((8, 512), F32),
            pltpu.VMEM((2, 1024, 256), BF16),
            pltpu.VMEM((2, 1024, 256), BF16),
            pltpu.VMEM((1024, 256), BF16),
            pltpu.VMEM((1024, 256), BF16),
            pltpu.VMEM((256, 1024), BF16),
            pltpu.VMEM((256, 1024), BF16),
            pltpu.VMEM((2, NZ, 8, 4096), F32),
            pltpu.VMEM((32, 128, 128), BF16),
            pltpu.VMEM((32, 128, 128), BF16),
            pltpu.VMEM((NC, 16, 128), F32),
            pltpu.VMEM((NC, 16, 128), F32),
            pltpu.VMEM((NY, 16, 128), F32),
            pltpu.VMEM((NX, 2, 16, 128), F32),
            pltpu.VMEM((2, 2, 8, 128), F32),
            pltpu.VMEM((NC, 2, 8, 128), F32),
            pltpu.VMEM((NZ, 8, 128), F32),
            pltpu.VMEM((NC, 2, 8, 128), F32),
            pltpu.VMEM((NC, 2, 8, 128), F32),
            pltpu.VMEM((NX, 2, 16, 128), F32),
            pltpu.VMEM((NY, 16, 128), F32),
            pltpu.VMEM((NY, 16, 128), F32),
            pltpu.VMEM((NY, 16, 128), F32),
            pltpu.VMEM((NX, 2, 8, 128), F32),
            pltpu.VMEM((NX, 2, 8, 128), F32),
            pltpu.VMEM((NX, 8, 128), F32),
            pltpu.VMEM((NX, 8, 128), F32),
            pltpu.VMEM((NC, 8, 128), F32),
            pltpu.SemaphoreType.DMA((9,)),
            pltpu.SemaphoreType.DMA((stages,)),
            pltpu.SemaphoreType.DMA((stages,)),
        ],
        compiler_params=pltpu.CompilerParams(collective_id=0, has_side_effects=True),
    )(update_map, leaf_rhs, leaf_inverse, update_rows, sep_rhs, sep_inverse)
    leaf, sep = pl.pallas_call(
        finish,
        name="finish",
        out_shape=(jax.ShapeDtypeStruct((2, 16, 64), F32), jax.ShapeDtypeStruct((8, 16), F32)),
        in_specs=[vmem, vmem],
        out_specs=(vmem, vmem),
    )(pltpu.with_memory_space_constraint(leaf, pltpu.VMEM), pltpu.with_memory_space_constraint(sep, pltpu.VMEM))
    return leaf, sep.T


def solution(mesh):
    in_specs = (
        P("leaf", None, "col"),
        P("leaf", "row", "col"),
        P("leaf", "col", "row"),
        P("leaf", None),
        P(),
        P(("leaf", "row", "col"), None),
    )
    out_specs = (P("leaf", None, ("col", "row")), P(None, ("leaf", "row", "col")))
    return jax.shard_map(body, mesh=mesh, in_specs=in_specs, out_specs=out_specs, check_vma=False)
```

time: 834 us -> 64.8 us (0.08)
  waiting for transfers between devices: 799 us -> 0 us
  Pallas kernels: 0 us -> 64.1 us
  between operations: 13.9 us -> 0.64 us
  matrix products: 11.6 us -> 0 us
    psum x4 -> x0, waiting for transfers between devices: 775 us -> none  [the longest x1 274 us: body(): total = lax.psum(contrib, ('leaf', 'row', 'col'))]
    pallas_call x0 -> x2, Pallas kernels: none -> 64.1 us  [the longest x1 63.4 us: body(): pl.pallas_call(kernel, name='substitution', out_shape=(pltpu.VMEM((2, 16,...]
    unnamed x6 -> x0, waiting for transfers between devices: 23.4 us -> none
    dot_general x8 -> x0, matrix products: 11.6 us -> none  [the longest x1 3.23 us: body(): jnp.einsum('sij,srj->sri', leaf_inverse, leaf_rhs, precision=HIGH)]
  transfers between devices with their start and end apart: 5 -> 0, of which waited for: 5 -> 0; matrix products, arithmetic and copies ran while one was open for 0% -> 0% of each run, Pallas kernels for 0% -> 0%
where the time goes in v3:
time: 64.8 us; the launch traced here: 64.7 us
  Pallas kernels  64.1 us (99%)
    pallas_call x1, Pallas kernels, body(): pl.pallas_call(kernel, name='substitution', out_shape=(pltpu.VMEM((2, 16,...  63.4 us

profile of v3, /device:TPU:1, one launch (start us, length us, event | category | flops | bytes accessed | tf_op | source)
XLA Modules:
  0.0 64.7 jit_solution(3487721750808792753)
XLA Ops:
  0.6 63.4 %substitution.1 = (f32[2,16,64]{2,1,0:T(8,128)S(1)}, f32[8,16]{1,0:T(8,128)S(1)}) custom-call(s32[2,16]{1,0:T(2,128)} %map_hbm.1, f32[2,16,256]{2,1,0:T(8,128)} %rhs_hbm.1, f32[2,1024,256]{2,1,0:T(8,128)} %l_hbm.1, f32[2,128,1024]{2,1,0:T(8,128)} %u_hbm.1, f32[16,4096]{1,0:T(8,128)} %srhs_hbm.1, f32[8,4096]{1,0:T(8,128)} %s_hbm.1), custom_call_target="tpu_custom_call" | custom-call | tf_op jit(solution)/shard_map/substitution/pallas_call | solution.py:307
  64.1 0.6 finish.1

commit v4 on v3

--- a/solution.py
+++ b/solution.py
@@ -11,14 +11,19 @@
 NT = (((1,), (1,)), ((), ()))
 NN = (((1,), (0,)), ((), ()))
 
-Y_STEPS = (4, 3, 5, 2, 6, 1, 7)
-COL_STEPS = [(dy, dc) for dy in Y_STEPS + (0,) for dc in (0, 1) if (dy, dc) != (0, 0)]
+Y_FAR = (4,)
+Y_NEAR = (3, 5, 2, 6, 1, 7)
+Y_STEPS = Y_FAR + Y_NEAR
+COL_FAR = [(4, 0), (4, 1)]
+COL_MID = [(dy, dc) for dy in (3, 5) for dc in (0, 1)]
+COL_NEAR = [(dy, dc) for dy in (2, 6, 1, 7) for dc in (0, 1)] + [(0, 1)]
+COL_STEPS = COL_FAR + COL_MID + COL_NEAR
 Z_STEPS = (4, 3, 5, 2, 6, 1, 7)
 X_STEPS = (2, 1, 3)
 MESH = pl.DeviceIdType.MESH
 
-(A_SUM, S_NEAR, A_GATHER, S_FAR, C_SUM, C_GATHER, S_SWAP, Z_SUM, D_SUM, U_SWAP, D_ROW, F_SUM, F_GATHER, G_SUM,
- L_SWAP, H_ROW, H_COL) = range(17)
+(A_SUM, S_1, S_2, S_3, S_1B, S_2B, S_3B, S_4, S_SWAP, U_SWAP, L_SWAP, A_FAR, A_NEAR, C_SUM, C_FAR, C_MID, C_NEAR, Z_SUM, D_SUM, D_ROW,
+ F_SUM, F_FAR, F_NEAR, G_SUM, H_ROW, H_COL) = range(26)
 
 
 def halves(a):
@@ -37,7 +42,7 @@
 def kernel(
     map_hbm, rhs_hbm, l_hbm, u_hbm, srhs_hbm, s_hbm, leaf_out, sep_out,
     map_ref, rhs_v, l_v, l_par, u_own, u_par, srhs_v, l_hi, l_lo, lp_hi, lp_lo, u_hi, u_lo, s_v, s_hi, s_lo,
-    part, a_rs, fwd, b1, b2s, b2, c_ar, bs, d_rs, e2, fs, f_rs, red, gs, g_rs, hs, h1, h2,
+    part, a_rs, fwd, b1, b2s, b2, c_ar, bs, d_rs, e2, fs, f_rs, red, gs, g_rs, hs, h1, h2, hold_a, hold_c, hold_f,
     load_sem, send_sem, recv_sem,
 ):
     z = lax.axis_index("leaf")
@@ -59,6 +64,12 @@
 
     def x_peer(step):
         return lax.rem(x + step, NX)
+
+    barrier = pltpu.get_barrier_semaphore()
+    peers = [{"col": col_peer(step)} for step in COL_STEPS]
+    peers += [{"leaf": z_peer(step)} for step in Z_STEPS]
+    peers += [{"row": x_peer(step)} for step in X_STEPS]
+    peers += [{"row": x_peer(step), "col": partner} for step in X_STEPS]
 
     s_here = pl.ds(pl.multiple_of(z * 512, 512), 512)
     loads = [
@@ -75,16 +86,12 @@
         pltpu.make_async_copy(srhs_hbm.at[pl.ds(pl.multiple_of(core * 8, 8), 8), s_here], srhs_v, load_sem.at[7]),
         pltpu.make_async_copy(map_hbm, map_ref, load_sem.at[8]),
     ]
-    for copy in loads:
+    for copy in loads[:5]:
         copy.start()
-
-    barrier = pltpu.get_barrier_semaphore()
-    peers = [{"col": col_peer(step)} for step in COL_STEPS]
-    peers += [{"leaf": z_peer(step)} for step in Z_STEPS]
-    peers += [{"row": x_peer(step)} for step in X_STEPS]
-    peers += [{"row": x_peer(step), "col": partner} for step in X_STEPS]
     for peer in peers:
         pl.semaphore_signal(barrier, inc=1, device_id=peer, device_id_type=MESH)
+    for copy in loads[5:]:
+        copy.start()
 
     def send(stage, src, dst, where):
         pltpu.make_async_remote_copy(
@@ -97,6 +104,12 @@
 
     def drained(stage, view):
         pltpu.make_async_copy(view, view, send_sem.at[stage]).wait()
+
+    def split_u(u, row):
+        for j in range(8):
+            hi, lo = halves(u[:, j * 128:(j + 1) * 128])
+            u_hi[j, row:row + 128] = hi
+            u_lo[j, row:row + 128] = lo
 
     loads[0].wait()
     for s in range(2):
@@ -114,88 +127,119 @@
     for step in COL_STEPS:
         peer = col_peer(step)
         send(A_SUM, part.at[peer], a_rs.at[me], {"col": peer})
+    left = pl.ds(0, 2048)
+    right = pl.ds(2048, 2048)
+
+    def ring(arrived, onward, columns, distance):
+        landed(arrived, s_v.at[0, pl.ds(0, 2), :, columns])
+        for step, to in ((distance, 7), (NZ - distance, 1)):
+            piece = s_v.at[core, z_peer(step), :, columns]
+            if distance < 3:
+                send(onward, piece, piece, {"leaf": z_peer(to)})
+            elif (columns is left) == (to == 1):
+                send(S_4, piece, piece, {"leaf": z_peer(to)})
+            send(S_SWAP, piece, piece, {"col": partner})
+
     send(U_SWAP, u_hbm.at[other], u_par, {"col": partner})
-    for step in (1, 7, 2, 6):
-        send(S_NEAR, s_hbm, s_v.at[core, z], {"leaf": z_peer(step)})
+    for stage, columns in ((S_1, left), (S_1B, right)):
+        for step in (1, 7):
+            send(stage, s_hbm.at[:, columns], s_v.at[core, z, :, columns], {"leaf": z_peer(step)})
     send(S_SWAP, s_hbm, s_v.at[core, z], {"col": partner})
     a_rs[me] = part[me]
     loads[5].wait()
-    hi, lo = halves(u_own[...])
-    u_hi[0:128] = hi
-    u_lo[0:128] = lo
+    split_u(u_own, 0)
     landed(U_SWAP, u_par)
-    hi, lo = halves(u_par[...])
-    u_hi[128:256] = hi
-    u_lo[128:256] = lo
+    split_u(u_par, 128)
+
+    ring(S_1, S_2, left, 1)
+    ring(S_1B, S_2B, right, 1)
 
     landed(A_SUM, a_rs.at[pl.ds(0, 15)])
     fwd[y] = jnp.sum(a_rs[...], axis=0)
-    for step in Y_STEPS:
-        send(A_GATHER, fwd.at[y], fwd.at[y], {"col": 2 * y_peer(step) + core})
+    for stage, steps in ((A_FAR, Y_FAR), (A_NEAR, Y_NEAR)):
+        for step in steps:
+            send(stage, fwd.at[y], fwd.at[y], {"col": 2 * y_peer(step) + core})
     send(L_SWAP, l_hbm.at[other], l_par, {"col": partner})
     loads[6].wait()
     loads[7].wait()
     loads[8].wait()
 
-    landed(A_GATHER, fwd.at[pl.ds(0, 7)])
-    f = jnp.concatenate([fwd[j] for j in range(8)], axis=1)
-    coupled = dot3(f, u_hi[...], u_lo[...], NT)
+    def u_rows(j):
+        return u_hi[j], u_lo[j]
+
+    def gathered(vectors, matrix, steps, dims):
+        chips = [y_peer(step) for step in steps]
+        v = jnp.concatenate([vectors[j] for j in chips], axis=1)
+        parts = [matrix(j) for j in chips]
+        axis = dims[0][1][0]
+        return dot3(
+            v, jnp.concatenate([p[0] for p in parts], axis=axis), jnp.concatenate([p[1] for p in parts], axis=axis), dims
+        )
+
+    ring(S_2, S_3, left, 2)
+    ring(S_2B, S_3B, right, 2)
+    landed(A_NEAR, fwd.at[pl.ds(0, 6)])
+    coupled = gathered(fwd, u_rows, (0,) + Y_NEAR, NT)
+    hold_a[...] = coupled
+    landed(A_FAR, fwd.at[pl.ds(0, 1)])
+    coupled = hold_a[...] + gathered(fwd, u_rows, Y_FAR, NT)
     for q in range(2):
         b1[x, q] = coupled[:, q * 128:(q + 1) * 128]
     for step in X_STEPS:
         send(C_SUM, b1.at[x], b1.at[x], {"row": x_peer(step)})
 
-    landed(S_NEAR, s_v.at[0, pl.ds(0, 4)])
-    below = z_peer(6)
-    above = z_peer(2)
-    send(S_FAR, s_v.at[core, below], s_v.at[core, below], {"leaf": z_peer(1)})
-    send(S_FAR, s_v.at[core, above], s_v.at[core, above], {"leaf": z_peer(7)})
-    left = pl.ds(0, 2048)
-    right = pl.ds(2048, 2048)
-    send(S_FAR, s_v.at[core, below, :, left], s_v.at[core, below, :, left], {"leaf": z_peer(2)})
-    send(S_FAR, s_v.at[core, above, :, right], s_v.at[core, above, :, right], {"leaf": z_peer(6)})
-    for step in (1, 7, 2, 6):
-        where = z_peer(step)
-        send(S_SWAP, s_v.at[core, where], s_v.at[core, where], {"col": partner})
+    ring(S_3, S_4, left, 3)
+    ring(S_3B, S_4, right, 3)
 
     landed(C_SUM, b1.at[pl.ds(0, 3)])
     total = jnp.sum(b1[...], axis=0)
     for h in range(2):
         for q in range(2):
             b2s[h, q] = total[q, 8 * h:8 * h + 8]
-    for step in COL_STEPS:
-        peer = col_peer(step)
-        send(C_GATHER, b2s.at[lax.rem(core + step[1], 2)], b2.at[me], {"col": peer})
+    for stage, steps in ((C_FAR, COL_FAR), (C_MID, COL_MID), (C_NEAR, COL_NEAR)):
+        for step in steps:
+            send(stage, b2s.at[lax.rem(core + step[1], 2)], b2.at[me], {"col": col_peer(step)})
     b2[me] = b2s[core]
 
-    landed(S_FAR, s_v.at[0, pl.ds(0, 3)])
-    for step in (3, 5, 4):
-        where = z_peer(step)
-        send(S_SWAP, s_v.at[core, where], s_v.at[core, where], {"col": partner})
+    landed(S_4, s_v.at[0, 0])
+    piece = s_v.at[core, z_peer(4)]
+    send(S_SWAP, piece, piece, {"col": partner})
+
+    def split_s(c):
+        rows = pl.ds(pl.multiple_of(c * 64, 64), 64)
+        for b in range(32):
+            hi, lo = halves(s_v[c, :, :, b * 128:(b + 1) * 128].reshape(64, 128))
+            s_hi[b, rows] = hi
+            s_lo[b, rows] = lo
+
+    split_s(core)
     landed(S_SWAP, s_v.at[0])
-    for b in range(32):
-        hi, lo = halves(s_v[:, :, :, b * 128:(b + 1) * 128].reshape(128, 128))
-        s_hi[b] = hi
-        s_lo[b] = lo
+    split_s(other)
 
     def block_pair(k):
-        c = k % 2
+        c = lax.rem(k, 2)
         return map_ref[c, k], map_ref[c, k + 1 - 2 * c]
 
-    def s_pair(ref, pair):
-        return jnp.concatenate([ref[pair[0]], ref[pair[1]]], axis=1)
-
-    acc = jnp.zeros((8, 128), F32)
-    for i in range(2):
-        pair = (4 * z + 2 * i, 4 * z + 2 * i + 1)
-        acc = acc + dot3(srhs_v[:, i * 256:(i + 1) * 256], s_pair(s_hi, pair), s_pair(s_lo, pair), NT)
-
-    landed(C_GATHER, b2.at[pl.ds(0, 15)])
-    for k in range(NC):
-        pair = block_pair(k)
-        raw = jnp.concatenate([b2[k, 0], b2[k, 1]], axis=1)
-        acc = acc - dot3(raw, s_pair(s_hi, pair), s_pair(s_lo, pair), NT)
-    c_ar[z] = acc
+    def s_join(ref, blocks):
+        return jnp.concatenate([ref[b] for b in blocks], axis=1)
+
+    def s_times(v, blocks, dims):
+        return dot3(v, s_join(s_hi, blocks), s_join(s_lo, blocks), dims)
+
+    here = [4 * z + i for i in range(4)]
+
+    def arrived_times_s(steps):
+        cols = [col_peer(step) for step in steps]
+        raw = jnp.concatenate([b2[k, q] for k in cols for q in range(2)], axis=1)
+        return s_times(raw, [b for k in cols for b in block_pair(k)], NT)
+
+    acc = s_times(srhs_v[...], here, NT)
+    landed(C_NEAR, b2.at[pl.ds(0, 9)])
+    hold_c[...] = acc - arrived_times_s([(0, 0)] + COL_NEAR)
+    landed(C_MID, b2.at[pl.ds(0, 4)])
+    hold_c[...] = hold_c[...] - arrived_times_s(COL_MID)
+    landed(C_FAR, b2.at[pl.ds(0, 2)])
+    c_ar[z] = hold_c[...] - arrived_times_s(COL_FAR)
     for step in Z_STEPS:
         send(Z_SUM, c_ar.at[z], c_ar.at[z], {"leaf": z_peer(step)})
     landed(L_SWAP, l_par)
@@ -205,20 +249,19 @@
     landed(Z_SUM, c_ar.at[pl.ds(0, 7)])
     sf = jnp.sum(c_ar[...], axis=0)
 
-    for k in range(NC):
-        pair = block_pair(k)
-        p = dot3(sf, s_pair(s_hi, pair), s_pair(s_lo, pair), NN)
-        bs[k, 0] = p[:, :128]
-        bs[k, 1] = p[:, 128:]
-    for step in COL_STEPS:
-        peer = col_peer(step)
-        send(D_SUM, bs.at[peer], d_rs.at[me], {"col": peer})
+    for steps in (COL_FAR + COL_MID, COL_NEAR + [(0, 0)]):
+        cols = [col_peer(step) for step in steps]
+        p = s_times(sf, [b for k in cols for b in block_pair(k)], NN)
+        for i, k in enumerate(cols):
+            bs[k, 0] = p[:, 256 * i:256 * i + 128]
+            bs[k, 1] = p[:, 256 * i + 128:256 * i + 256]
+        for step, k in zip(steps, cols):
+            if step != (0, 0):
+                send(D_SUM, bs.at[k], d_rs.at[me], {"col": k})
     d_rs[me] = bs[me]
-    for i in range(2):
-        pair = (4 * z + 2 * i, 4 * z + 2 * i + 1)
-        p = dot3(sf, s_pair(s_hi, pair), s_pair(s_lo, pair), NN)
-        hs[2 * i] = p[:, :128]
-        hs[2 * i + 1] = p[:, 128:]
+    p = s_times(sf, here, NN)
+    for i in range(4):
+        hs[i] = p[:, 128 * i:128 * i + 128]
     for step in X_STEPS:
         peer = x_peer(step)
         send(H_ROW, hs.at[peer], h1.at[x], {"row": peer})
@@ -239,7 +282,10 @@
         send(H_COL, h2.at[me], h2.at[me], {"col": col_peer(step)})
     landed(D_ROW, e2.at[pl.ds(0, 3)])
     pulled = jnp.sum(e2[...], axis=0)
-    p = dot3(jnp.concatenate([pulled[0], pulled[1]], axis=1), u_hi[...], u_lo[...], NN)
+    p = dot3(
+        jnp.concatenate([pulled[0], pulled[1]], axis=1),
+        jnp.concatenate([u_hi[j] for j in range(8)], axis=1), jnp.concatenate([u_lo[j] for j in range(8)], axis=1), NN,
+    )
     for j in range(8):
         fs[j] = p[:, j * 128:(j + 1) * 128]
     for step in Y_STEPS:
@@ -257,12 +303,24 @@
     sep_out[...] = jnp.transpose(pltpu.roll(block, lax.rem(128 - 8 * me, 128), 1))[:8]
     landed(F_SUM, f_rs.at[pl.ds(0, 7)])
     red[y] = fwd[y] - jnp.sum(f_rs[...], axis=0)
-    for step in Y_STEPS:
-        send(F_GATHER, red.at[y], red.at[y], {"col": 2 * y_peer(step) + core})
-    landed(F_GATHER, red.at[pl.ds(0, 7)])
-    f = jnp.concatenate([red[j] for j in range(8)], axis=1)
-    for where, mine in ((other, False), (core, True)):
-        p = dot3(f, l_hi[core], l_lo[core], NN) if mine else dot3(f, lp_hi[...], lp_lo[...], NN)
+    for stage, steps in ((F_FAR, Y_FAR), (F_NEAR, Y_NEAR)):
+        for step in steps:
+            send(stage, red.at[y], red.at[y], {"col": 2 * y_peer(step) + core})
+
+    def l_partner(j):
+        rows = pl.ds(pl.multiple_of(j * 128, 128), 128)
+        return lp_hi[rows], lp_lo[rows]
+
+    def l_own(j):
+        rows = pl.ds(pl.multiple_of(j * 128, 128), 128)
+        return l_hi[core, rows], l_lo[core, rows]
+
+    landed(F_NEAR, red.at[pl.ds(0, 6)])
+    for i, matrix in enumerate((l_partner, l_own)):
+        hold_f[i] = gathered(red, matrix, (0,) + Y_NEAR, NN)
+    landed(F_FAR, red.at[pl.ds(0, 1)])
+    for where, mine, matrix in ((other, False, l_partner), (core, True, l_own)):
+        p = hold_f[int(mine)] + gathered(red, matrix, Y_FAR, NN)
         for k in range(NX):
             piece = p[:, k * 64:(k + 1) * 64]
             gs[k, where] = jnp.concatenate([piece[:8], piece[8:]], axis=1)
@@ -272,19 +330,26 @@
     send(G_SUM, gs.at[x, other], g_rs.at[x, core], {"col": partner})
     g_rs[x, core] = gs[x, core]
     drained(A_SUM, part.at[pl.ds(0, 15)])
-    drained(S_NEAR, s_v.at[0, pl.ds(0, 4)])
-    drained(A_GATHER, fwd.at[pl.ds(0, 7)])
-    drained(S_FAR, s_v.at[0, pl.ds(0, 3)])
+    for stage in (S_1, S_2, S_3):
+        drained(stage, s_v.at[0, pl.ds(0, 2), :, left])
+    for stage in (S_1B, S_2B, S_3B):
+        drained(stage, s_v.at[0, pl.ds(0, 2), :, right])
+    drained(S_4, s_v.at[0, 0])
+    drained(S_SWAP, s_v.at[0])
+    drained(U_SWAP, u_par)
+    drained(L_SWAP, l_par)
+    drained(A_FAR, fwd.at[pl.ds(0, 1)])
+    drained(A_NEAR, fwd.at[pl.ds(0, 6)])
     drained(C_SUM, b1.at[pl.ds(0, 3)])
-    drained(C_GATHER, b2.at[pl.ds(0, 15)])
-    drained(S_SWAP, s_v.at[0])
+    drained(C_FAR, b2.at[pl.ds(0, 2)])
+    drained(C_MID, b2.at[pl.ds(0, 4)])
+    drained(C_NEAR, b2.at[pl.ds(0, 9)])
     drained(Z_SUM, c_ar.at[pl.ds(0, 7)])
     drained(D_SUM, d_rs.at[pl.ds(0, 15)])
-    drained(U_SWAP, u_par)
     drained(D_ROW, e2.at[pl.ds(0, 3)])
     drained(F_SUM, fs.at[pl.ds(0, 7)])
-    drained(F_GATHER, red.at[pl.ds(0, 7)])
-    drained(L_SWAP, l_par)
+    drained(F_FAR, red.at[pl.ds(0, 1)])
+    drained(F_NEAR, red.at[pl.ds(0, 6)])
     drained(H_ROW, h1.at[pl.ds(0, 3)])
     drained(H_COL, h2.at[pl.ds(0, 15)])
     landed(G_SUM, c_ar.at[pl.ds(0, 7)])
@@ -303,7 +368,7 @@
 def body(leaf_rhs, leaf_inverse, update_rows, update_map, sep_rhs, sep_inverse):
     hbm = pl.BlockSpec(memory_space=pl.ANY)
     vmem = pl.BlockSpec(memory_space=pltpu.VMEM)
-    stages = 17
+    stages = 26
     leaf, sep = pl.pallas_call(
         kernel,
         name="substitution",
@@ -322,8 +387,8 @@
             pltpu.VMEM((2, 1024, 256), BF16),
             pltpu.VMEM((1024, 256), BF16),
             pltpu.VMEM((1024, 256), BF16),
-            pltpu.VMEM((256, 1024), BF16),
-            pltpu.VMEM((256, 1024), BF16),
+            pltpu.VMEM((NY, 256, 128), BF16),
+            pltpu.VMEM((NY, 256, 128), BF16),
             pltpu.VMEM((2, NZ, 8, 4096), F32),
             pltpu.VMEM((32, 128, 128), BF16),
             pltpu.VMEM((32, 128, 128), BF16),
@@ -345,6 +410,9 @@
             pltpu.VMEM((NX, 8, 128), F32),
             pltpu.VMEM((NX, 8, 128), F32),
             pltpu.VMEM((NC, 8, 128), F32),
+            pltpu.VMEM((16, 256), F32),
+            pltpu.VMEM((8, 128), F32),
+            pltpu.VMEM((2, 16, 256), F32),
             pltpu.SemaphoreType.DMA((9,)),
             pltpu.SemaphoreType.DMA((stages,)),
             pltpu.SemaphoreType.DMA((stages,)),

time: 64.8 us -> 64.1 us (0.989)
  Pallas kernels: 64.1 us -> 63.3 us
    pallas_call x1, Pallas kernels: 63.4 us -> 62.7 us  [body(): pl.pallas_call(kernel, name='substitution', out_shape=(pltpu.VMEM((2, 16,...]
where the time goes in v4:
time: 64.1 us; the launch traced here: 63.9 us
  Pallas kernels  63.3 us (99%)
    pallas_call x1, Pallas kernels, body(): pl.pallas_call(kernel, name='substitution', out_shape=(pltpu.VMEM((2, 16,...  62.7 us

profile of v4, /device:TPU:1, one launch (start us, length us, event | category | flops | bytes accessed | tf_op | source)
XLA Modules:
  0.0 63.9 jit_solution(4855734190291809877)
XLA Ops:
  0.6 62.7 %substitution.1 = (f32[2,16,64]{2,1,0:T(8,128)S(1)}, f32[8,16]{1,0:T(8,128)S(1)}) custom-call(s32[2,16]{1,0:T(2,128)} %map_hbm.1, f32[2,16,256]{2,1,0:T(8,128)} %rhs_hbm.1, f32[2,1024,256]{2,1,0:T(8,128)} %l_hbm.1, f32[2,128,1024]{2,1,0:T(8,128)} %u_hbm.1, f32[16,4096]{1,0:T(8,128)} %srhs_hbm.1, f32[8,4096]{1,0:T(8,128)} %s_hbm.1), custom_call_target="tpu_custom_call" | custom-call | tf_op jit(solution)/shard_map/substitution/pallas_call | solution.py:372
  63.3 0.6 finish.1

commit v5 on v4

v5 whole, which is shorter than its diff:
```python
import jax
import jax.numpy as jnp
from jax import lax
from jax.experimental import pallas as pl
from jax.experimental.pallas import tpu as pltpu
from jax.sharding import PartitionSpec as P

NZ, NX, NC, NY = 8, 4, 16, 8
F32 = jnp.float32
BF16 = jnp.bfloat16
NT = (((1,), (1,)), ((), ()))
NN = (((1,), (0,)), ((), ()))

Y_GROUPS = ((4,), (3, 5, 2, 6, 1, 7))
Y_STEPS = sum(Y_GROUPS, ())
COL_GROUPS = [[(dy, dc) for dy in steps for dc in (0, 1) if (dy, dc) != (0, 0)] for steps in ((4,), (3, 5, 2, 6, 1, 7, 0))]
COL_STEPS = sum(COL_GROUPS, [])
Z_STEPS = (4, 3, 5, 2, 6, 1, 7)
X_STEPS = (2, 1, 3)
MESH = pl.DeviceIdType.MESH

(A_SUM, S_OWN, S_4, S_SWAP, U_SWAP, L_SWAP, C_SUM, Z_SUM, D_SUM, D_ROW, F_SUM, G_SUM, H_ROW, H_COL) = range(14)
A_GATHER = 14
F_GATHER = 16
C_GATHER = 18
S_RING = 20
STAGES = 32
TILES = 1059


def halves(a):
    hi = a.astype(BF16)
    return hi, (a - hi.astype(F32)).astype(BF16)


def dot3(a, b_hi, b_lo, dims):
    m = a.shape[0]
    a_hi, a_lo = halves(a)
    both = lax.dot_general(jnp.concatenate([a_hi, a_lo], axis=0), b_hi, dims, preferred_element_type=F32)
    rest = lax.dot_general(a_hi, b_lo, dims, preferred_element_type=F32)
    return both[:m] + (both[m:] + rest)


def kernel(
    map_hbm, rhs_hbm, l_hbm, u_hbm, srhs_hbm, s_hbm, leaf_out, sep_out,
    map_ref, rhs_v, l_v, l_par, u_own, u_par, srhs_v, l_hi, l_lo, lp_hi, lp_lo, u_hi, u_lo, ut_hi, ut_lo, s_v, s_hi, s_lo, st_hi, st_lo,
    part, a_rs, fwd, b1, b2s, b2, c_ar, bs, d_rs, e2, fs, f_rs, red, gs, g_rs, hs, h1, h2, hold_a, hold_c, hold_f, tally,
    load_sem, send_sem, recv_sem,
):
    z = lax.axis_index("leaf")
    x = lax.axis_index("row")
    me = lax.axis_index("col")
    y = me // 2
    core = me % 2
    other = 1 - core
    partner = 2 * y + other

    def col_peer(step):
        return lax.rem(y + step[0], NY) * 2 + lax.rem(core + step[1], 2)

    def y_peer(step):
        return lax.rem(y + step, NY)

    def z_peer(step):
        return lax.rem(z + step, NZ)

    def x_peer(step):
        return lax.rem(x + step, NX)

    barrier = pltpu.get_barrier_semaphore()
    peers = [{"leaf": z_peer(step)} for step in (4, 3, 5)]
    peers += [{"col": col_peer(step)} for step in COL_STEPS]
    peers += [{"row": x_peer(step)} for step in X_STEPS]
    peers += [{"row": x_peer(step), "col": partner} for step in X_STEPS]
    peers += [{"leaf": z_peer(step)} for step in (2, 6, 1, 7)]
    for peer in peers:
        pl.semaphore_signal(barrier, inc=1, device_id=peer, device_id_type=MESH)

    s_here = pl.ds(pl.multiple_of(z * 512, 512), 512)
    loads = [
        pltpu.make_async_copy(rhs_hbm, rhs_v, load_sem.at[0]),
        *(
            pltpu.make_async_copy(
                l_hbm.at[s, pl.ds(h * 512, 512)], l_v.at[s, pl.ds(h * 512, 512)], load_sem.at[1 + 2 * s + h]
            )
            for s in range(2)
            for h in range(2)
        ),
        pltpu.make_async_copy(u_hbm.at[core], u_own, load_sem.at[5]),
        pltpu.make_async_copy(s_hbm, s_v.at[z, core], load_sem.at[6]),
        pltpu.make_async_copy(srhs_hbm.at[pl.ds(pl.multiple_of(core * 8, 8), 8), s_here], srhs_v, load_sem.at[7]),
        pltpu.make_async_copy(map_hbm, map_ref, load_sem.at[8]),
    ]
    for copy in loads:
        copy.start()

    def send(stage, src, dst, where):
        pltpu.make_async_remote_copy(
            src_ref=src, dst_ref=dst, send_sem=send_sem.at[0], recv_sem=recv_sem.at[stage],
            device_id=where, device_id_type=MESH,
        ).start()

    def landed(stage, view):
        pltpu.make_async_copy(view, view, recv_sem.at[stage]).wait()

    def split_u(u, row):
        for j in range(8):
            hi, lo = halves(u[:, j * 128:(j + 1) * 128])
            u_hi[j, row:row + 128] = hi
            u_lo[j, row:row + 128] = lo
            hi, lo = halves(jnp.transpose(u[:, j * 128:(j + 1) * 128]))
            ut_hi[j, :, row:row + 128] = hi
            ut_lo[j, :, row:row + 128] = lo

    loads[0].wait()
    for s in range(2):
        for h in range(2):
            loads[1 + 2 * s + h].wait()
            rows = pl.ds(h * 512, 512)
            hi, lo = halves(l_v[s, rows])
            l_hi[s, rows] = hi
            l_lo[s, rows] = lo
            p = dot3(rhs_v[s], hi, lo, NT)
            for j in range(4):
                part[2 * (4 * h + j) + s] = p[:, j * 128:(j + 1) * 128]

    pl.semaphore_wait(barrier, len(peers))
    for step in COL_STEPS:
        peer = col_peer(step)
        send(A_SUM, part.at[peer], a_rs.at[me], {"col": peer})
    onward = lax.rem(z + 2 * core + 7, NZ)
    halved = (pl.ds(0, 2048), pl.ds(2048, 2048))
    pieces = [(owner, columns) for owner in (core, other) for columns in halved]

    def behind(distance):
        return lax.rem(z + NZ + distance * (1 - 2 * core), NZ)

    def ring(distance, i):
        stage = S_RING + 4 * (distance - 1) + i
        owner, columns = pieces[i]
        piece = s_v.at[behind(distance), owner, :, columns]
        landed(stage, s_v.at[0, 0, :, halved[0]])
        if distance < 3:
            send(stage + 4, piece, piece, {"leaf": onward})
        elif i % 2 == 1:
            last_step(owner)
        send(S_SWAP, piece, piece, {"col": partner})

    def last_step(owner):
        piece = s_v.at[behind(3), owner, :, pl.ds(pl.multiple_of(2048 * core, 2048), 2048)]
        send(S_4, piece, piece, {"leaf": onward})

    send(S_OWN, s_hbm, s_v.at[z, core], {"col": partner})
    for i in range(2):
        columns = halved[i]
        send(S_RING + i, s_hbm.at[:, columns], s_v.at[z, core, :, columns], {"leaf": onward})
    send(U_SWAP, u_hbm.at[other], u_par, {"col": partner})
    a_rs[me] = part[me]
    loads[5].wait()
    split_u(u_own, 0)
    landed(S_OWN, s_v.at[0, 0])
    for i in range(2):
        piece = s_v.at[z, other, :, halved[i]]
        send(S_RING + 2 + i, piece, piece, {"leaf": onward})
    landed(U_SWAP, u_par)
    split_u(u_par, 128)

    for i in range(4):
        ring(1, i)

    landed(A_SUM, a_rs.at[pl.ds(0, 15)])
    fwd[y] = jnp.sum(a_rs[...], axis=0)
    for i, steps in enumerate(Y_GROUPS):
        for step in steps:
            send(A_GATHER + i, fwd.at[y], fwd.at[y], {"col": 2 * y_peer(step) + core})
    loads[6].wait()
    loads[7].wait()
    loads[8].wait()

    def u_columns(j):
        return ut_hi[j], ut_lo[j]

    def gathered(vectors, matrix, steps):
        chips = [y_peer(step) for step in steps]
        v = jnp.concatenate([vectors[j] for j in chips], axis=1)
        parts = [matrix(j) for j in chips]
        return dot3(v, *(jnp.concatenate([p[i] for p in parts], axis=0) for i in range(2)), NN)

    for i in range(4):
        ring(2, i)
    landed(A_GATHER + 1, fwd.at[pl.ds(0, 6)])
    hold_a[...] = gathered(fwd, u_columns, (0,) + Y_GROUPS[1])
    landed(A_GATHER, fwd.at[0])
    coupled = hold_a[...] + gathered(fwd, u_columns, Y_GROUPS[0])
    for q in range(2):
        b1[x, q] = coupled[:, q * 128:(q + 1) * 128]
    for step in X_STEPS:
        send(C_SUM, b1.at[x], b1.at[x], {"row": x_peer(step)})

    for i in range(4):
        ring(3, i)

    landed(C_SUM, b1.at[pl.ds(0, 3)])
    total = jnp.sum(b1[...], axis=0)
    for h in range(2):
        for q in range(2):
            b2s[h, q] = total[q, 8 * h:8 * h + 8]
    for i, steps in enumerate(COL_GROUPS):
        for step in steps:
            send(C_GATHER + i, b2s.at[lax.rem(core + step[1], 2)], b2.at[me], {"col": col_peer(step)})
    b2[me] = b2s[core]

    def split_s(where):
        rows = pl.ds(pl.multiple_of(where * 16, 16), 16)
        for b in range(32):
            hi, lo = halves(s_v[where, :, :, b * 128:(b + 1) * 128].reshape(16, 128))
            s_hi[b, rows] = hi
            s_lo[b, rows] = lo

    for distance in range(4):
        split_s(behind(distance))
    landed(S_4, s_v.at[0, 0])
    piece = s_v.at[behind(4), :, :, pl.ds(pl.multiple_of(2048 * core, 2048), 2048)]
    send(S_SWAP, piece, piece, {"col": partner})
    landed(S_SWAP, s_v.at[pl.ds(0, 7), 0])
    for distance in range(4, 8):
        split_s(behind(distance))
    for b in range(32):
        hi, lo = halves(jnp.transpose(s_v[:, :, :, b * 128:(b + 1) * 128].reshape(128, 128)))
        st_hi[b] = hi
        st_lo[b] = lo

    def block_pair(k):
        c = lax.rem(k, 2)
        return map_ref[c, k], map_ref[c, k + 1 - 2 * c]

    def join(ref, blocks, axis):
        return jnp.concatenate([ref[b] for b in blocks], axis=axis)

    def times_st(v, blocks):
        return dot3(v, join(st_hi, blocks, 0), join(st_lo, blocks, 0), NN)

    def times_s(v, blocks):
        return dot3(v, join(s_hi, blocks, 1), join(s_lo, blocks, 1), NN)

    here = [4 * z + i for i in range(4)]

    def arrived_times_s(steps):
        cols = [col_peer(step) for step in steps]
        raw = jnp.concatenate([b2[k, q] for k in cols for q in range(2)], axis=1)
        return times_st(raw, [b for k in cols for b in block_pair(k)])

    hold_c[...] = times_st(srhs_v[...], here) - arrived_times_s([(0, 0)])
    for i, steps in reversed(list(enumerate(COL_GROUPS))):
        landed(C_GATHER + i, b2.at[pl.ds(0, len(steps))])
        hold_c[...] = hold_c[...] - arrived_times_s(steps)
    c_ar[z] = hold_c[...]
    for step in Z_STEPS:
        send(Z_SUM, c_ar.at[z], c_ar.at[z], {"leaf": z_peer(step)})
    send(L_SWAP, l_hbm.at[other], l_par, {"col": partner})
    landed(Z_SUM, c_ar.at[pl.ds(0, 7)])
    sf = jnp.sum(c_ar[...], axis=0)

    for steps in (COL_STEPS[:6], COL_STEPS[6:] + [(0, 0)]):
        cols = [col_peer(step) for step in steps]
        p = times_s(sf, [b for k in cols for b in block_pair(k)])
        for i, k in enumerate(cols):
            bs[k, 0] = p[:, 256 * i:256 * i + 128]
            bs[k, 1] = p[:, 256 * i + 128:256 * i + 256]
        for step, k in zip(steps, cols):
            if step != (0, 0):
                send(D_SUM, bs.at[k], d_rs.at[me], {"col": k})
    d_rs[me] = bs[me]
    p = times_s(sf, here)
    for i in range(4):
        hs[i] = p[:, 128 * i:128 * i + 128]
    for step in X_STEPS:
        peer = x_peer(step)
        send(H_ROW, hs.at[peer], h1.at[x], {"row": peer})
    h1[x] = hs[x]
    landed(H_ROW, h1.at[pl.ds(0, 3)])
    h2[me] = jnp.sum(h1[...], axis=0)

    landed(L_SWAP, l_par)
    hi, lo = halves(l_par[...])
    lp_hi[...] = hi
    lp_lo[...] = lo
    landed(D_SUM, d_rs.at[pl.ds(0, 15)])
    for h in range(2):
        half = d_rs[h]
        for k in range(1, NY):
            half = half + d_rs[2 * k + h]
        for q in range(2):
            e2[x, q, 8 * h:8 * h + 8] = half[q]
    for step in X_STEPS:
        send(D_ROW, e2.at[x], e2.at[x], {"row": x_peer(step)})
    for step in COL_STEPS:
        send(H_COL, h2.at[me], h2.at[me], {"col": col_peer(step)})
    landed(D_ROW, e2.at[pl.ds(0, 3)])
    pulled = jnp.sum(e2[...], axis=0)
    p = dot3(
        jnp.concatenate([pulled[0], pulled[1]], axis=1),
        jnp.concatenate([u_hi[j] for j in range(8)], axis=1), jnp.concatenate([u_lo[j] for j in range(8)], axis=1), NN,
    )
    for j in range(8):
        fs[j] = p[:, j * 128:(j + 1) * 128]
    for step in Y_STEPS:
        peer = y_peer(step)
        send(F_SUM, fs.at[peer], f_rs.at[y], {"col": 2 * peer + core})
    f_rs[y] = fs[y]
    landed(H_COL, h2.at[pl.ds(0, 15)])
    block = []
    for h in range(2):
        half = h2[h]
        for k in range(1, NY):
            half = half + h2[2 * k + h]
        block.append(half)
    block = jnp.concatenate(block, axis=0)
    sep_out[...] = jnp.transpose(pltpu.roll(block, lax.rem(128 - 8 * me, 128), 1))[:8]
    landed(F_SUM, f_rs.at[pl.ds(0, 7)])
    red[y] = fwd[y] - jnp.sum(f_rs[...], axis=0)
    for i, steps in enumerate(Y_GROUPS):
        for step in steps:
            send(F_GATHER + i, red.at[y], red.at[y], {"col": 2 * y_peer(step) + core})

    def l_partner(j):
        rows = pl.ds(pl.multiple_of(j * 128, 128), 128)
        return lp_hi[rows], lp_lo[rows]

    def l_own(j):
        rows = pl.ds(pl.multiple_of(j * 128, 128), 128)
        return l_hi[core, rows], l_lo[core, rows]

    matrices = (l_partner, l_own)
    landed(F_GATHER + 1, red.at[pl.ds(0, 6)])
    for i, matrix in enumerate(matrices):
        hold_f[i] = gathered(red, matrix, (0,) + Y_GROUPS[1])
    landed(F_GATHER, red.at[0])
    for i, (where, matrix) in enumerate(((other, l_partner), (core, l_own))):
        p = hold_f[i] + gathered(red, matrix, Y_GROUPS[0])
        gs[0, where] = p[:, :128]
        gs[1, where] = p[:, 128:]
        for step in X_STEPS:
            peer = x_peer(step)
            to = {"row": peer} if i == 1 else {"row": peer, "col": partner}
            send(G_SUM, gs.at[peer // 2, where], g_rs.at[x, core], to)
    send(G_SUM, gs.at[x // 2, other], g_rs.at[x, core], {"col": partner})
    g_rs[x, core] = gs[x // 2, core]
    landed(G_SUM, fs.at[pl.ds(0, 7)])
    total = jnp.sum(g_rs[...], axis=0)
    for s in range(2):
        leaf_out[s] = jnp.where(lax.rem(x, 2) == 0, total[s][:, :64], total[s][:, 64:])
    pltpu.make_async_copy(tally, tally, send_sem.at[0]).wait()


def finish(leaf_in, sep_in, leaf_out, sep_out):
    leaf_out[...] = leaf_in[...]
    sep_out[...] = sep_in[...]


def body(leaf_rhs, leaf_inverse, update_rows, update_map, sep_rhs, sep_inverse):
    hbm = pl.BlockSpec(memory_space=pl.ANY)
    vmem = pl.BlockSpec(memory_space=pltpu.VMEM)
    leaf, sep = pl.pallas_call(
        kernel,
        name="substitution",
        out_shape=(pltpu.VMEM((2, 16, 64), F32), pltpu.VMEM((8, 16), F32)),
        in_specs=[hbm, hbm, hbm, hbm, hbm, hbm],
        out_specs=(vmem, vmem),
        scratch_shapes=[
            pltpu.SMEM((2, 16), jnp.int32),
            pltpu.VMEM((2, 16, 256), F32),
            pltpu.VMEM((2, 1024, 256), F32),
            pltpu.VMEM((1024, 256), F32),
            pltpu.VMEM((128, 1024), F32),
            pltpu.VMEM((128, 1024), F32),
            pltpu.VMEM((8, 512), F32),
            pltpu.VMEM((2, 1024, 256), BF16),
            pltpu.VMEM((2, 1024, 256), BF16),
            pltpu.VMEM((1024, 256), BF16),
            pltpu.VMEM((1024, 256), BF16),
            pltpu.VMEM((NY, 256, 128), BF16),
            pltpu.VMEM((NY, 256, 128), BF16),
            pltpu.VMEM((NY, 128, 256), BF16),
            pltpu.VMEM((NY, 128, 256), BF16),
            pltpu.VMEM((NZ, 2, 8, 4096), F32),
            pltpu.VMEM((32, 128, 128), BF16),
            pltpu.VMEM((32, 128, 128), BF16),
            pltpu.VMEM((32, 128, 128), BF16),
            pltpu.VMEM((32, 128, 128), BF16),
            pltpu.VMEM((NC, 16, 128), F32),
            pltpu.VMEM((NC, 16, 128), F32),
            pltpu.VMEM((NY, 16, 128), F32),
            pltpu.VMEM((NX, 2, 16, 128), F32),
            pltpu.VMEM((2, 2, 8, 128), F32),
            pltpu.VMEM((NC, 2, 8, 128), F32),
            pltpu.VMEM((NZ, 8, 128), F32),
            pltpu.VMEM((NC, 2, 8, 128), F32),
            pltpu.VMEM((NC, 2, 8, 128), F32),
            pltpu.VMEM((NX, 2, 16, 128), F32),
            pltpu.VMEM((NY, 16, 128), F32),
            pltpu.VMEM((NY, 16, 128), F32),
            pltpu.VMEM((NY, 16, 128), F32),
            pltpu.VMEM((2, 2, 16, 128), F32),
            pltpu.VMEM((NX, 2, 16, 128), F32),
            pltpu.VMEM((NX, 8, 128), F32),
            pltpu.VMEM((NX, 8, 128), F32),
            pltpu.VMEM((NC, 8, 128), F32),
            pltpu.VMEM((16, 256), F32),
            pltpu.VMEM((8, 128), F32),
            pltpu.VMEM((2, 16, 256), F32),
            pltpu.VMEM((TILES, 8, 128), F32),
            pltpu.SemaphoreType.DMA((9,)),
            pltpu.SemaphoreType.DMA((1,)),
            pltpu.SemaphoreType.DMA((STAGES,)),
        ],
        compiler_params=pltpu.CompilerParams(collective_id=0, has_side_effects=True),
    )(update_map, leaf_rhs, leaf_inverse, update_rows, sep_rhs, sep_inverse)
    leaf, sep = pl.pallas_call(
        finish,
        name="finish",
        out_shape=(jax.ShapeDtypeStruct((2, 16, 64), F32), jax.ShapeDtypeStruct((8, 16), F32)),
        in_specs=[vmem, vmem],
        out_specs=(vmem, vmem),
    )(pltpu.with_memory_space_constraint(leaf, pltpu.VMEM), pltpu.with_memory_space_constraint(sep, pltpu.VMEM))
    return leaf, sep.T


def solution(mesh):
    in_specs = (
        P("leaf", None, "col"),
        P("leaf", "row", "col"),
        P("leaf", "col", "row"),
        P("leaf", None),
        P(),
        P(("leaf", "row", "col"), None),
    )
    out_specs = (P("leaf", None, ("col", "row")), P(None, ("leaf", "row", "col")))
    return jax.shard_map(body, mesh=mesh, in_specs=in_specs, out_specs=out_specs, check_vma=False)
```

time: 64.1 us -> 62.6 us (0.977)
  Pallas kernels: 63.3 us -> 61.8 us
    pallas_call x1, Pallas kernels: 62.7 us -> 61.2 us  [body(): pl.pallas_call(kernel, name='substitution', out_shape=(pltpu.VMEM((2, 16,...]
where the time goes in v5:
time: 62.6 us; the launch traced here: 62.4 us
  Pallas kernels  61.8 us (99%)
  between operations  0.64 us (1%)
    pallas_call x1, Pallas kernels, body(): pl.pallas_call(kernel, name='substitution', out_shape=(pltpu.VMEM((2, 16,...  61.2 us

profile of v5, /device:TPU:1, one launch (start us, length us, event | category | flops | bytes accessed | tf_op | source)
XLA Modules:
  0.0 62.4 jit_solution(14340186903270452822)
XLA Ops:
  0.6 61.2 %substitution.1 = (f32[2,16,64]{2,1,0:T(8,128)S(1)}, f32[8,16]{1,0:T(8,128)S(1)}) custom-call(s32[2,16]{1,0:T(2,128)} %map_hbm.1, f32[2,16,256]{2,1,0:T(8,128)} %rhs_hbm.1, f32[2,1024,256]{2,1,0:T(8,128)} %l_hbm.1, f32[2,128,1024]{2,1,0:T(8,128)} %u_hbm.1, f32[16,4096]{1,0:T(8,128)} %srhs_hbm.1, f32[8,4096]{1,0:T(8,128)} %s_hbm.1), custom_call_target="tpu_custom_call" | custom-call | tf_op jit(solution)/shard_map/substitution/pallas_call | solution.py:364
  61.8 0.6 finish.1
